TPU v7x, 256 devices: a whole 4x4x8 slice. The times are simulated.
256 devices in a mesh: samp: 4 (over y_lo, core), snp: 64 (over x, z, y_hi).
Axes of the slice: x: 4, y: 4 (y_hi: 2, y_lo: 2; y = y_hi * 2 + y_lo), z: 8, core: 2. Of those that a mesh axis runs over, the one named last changes fastest.
Arguments:
- dosage: int32 [3072, 2048], P('snp', 'samp'), may hold values from 0 to 2
- pheno: bfloat16 [2048, 2048], P('samp'), may hold values from -6 to 6
- perm: int32 [8, 2048], P(None, 'samp'), may hold values from 0 to 2047, each once within a row
- snp_weight: float32 [3072], P('snp'), may hold values from 0.015 to 64
Outputs:
- whitened: bfloat16 [9, 3072, 2048], P(None, 'snp', 'samp')
Inputs may be any that keep to these rules, and one draw needn't show every extreme that they name: `perm`: each of the 8 rows names every sample index exactly once.
All inputs are finite; a program needn't handle non-finite values.
Results may differ from a plain program's by a relative error of at most 0.012.
Values may be sent and summed in bfloat16 or wider, within the bound.
A program may use at most 64 MiB of HBM per device.

v0:
```python
import jax
import jax.numpy as jnp
from jax import lax
from jax.sharding import Mesh
from jax.sharding import PartitionSpec as P

SNP = ("snp_0", "snp_1", "snp_2")


def laid_out(parts, dim):
    dims = list(parts.shape[1:])
    dims[dim] *= parts.shape[0]
    return jnp.moveaxis(parts, 0, dim).reshape(dims)


def copy_for_each(array, axis):
    devices = lax.axis_size(axis)
    return lax.all_to_all(
        jnp.broadcast_to(array[None], (devices, *array.shape)), axis, 0, 0, tiled=True
    )


def gathered_copies(array, axis, dim):
    return laid_out(copy_for_each(array, axis), dim)


def cut_along(array, dim, devices):
    dims = array.shape
    parts = array.reshape(*dims[:dim], devices, dims[dim] // devices, *dims[dim + 1 :])
    return jnp.moveaxis(parts, dim, 0)


def sent_and_summed(array, axis, dim):
    parts = cut_along(array, dim, lax.axis_size(axis))
    arrived = lax.all_to_all(parts, axis, split_axis=0, concat_axis=0, tiled=True)
    return arrived.sum(axis=0)


def over_copies(array, axis):
    return copy_for_each(array, axis).sum(axis=0)


def together(arrays, axis):
    ends = [0]
    for a in arrays:
        ends.append(ends[-1] + a.size)
    so_far = over_copies(jnp.concatenate([a.ravel() for a in arrays]), axis)
    return tuple((so_far[b:e].reshape(a.shape) for a, b, e in zip(arrays, ends, ends[1:])))


def summed_rows(so_far, axes):
    for axis in axes:
        so_far = lax.psum_scatter(so_far, axis, scatter_dimension=0, tiled=True)
    return so_far


def product(left_block, right_block):
    rows_full = gathered_copies(left_block, "samp", 1)
    return jnp.dot(
        rows_full,
        lax.all_gather(right_block, SNP, axis=0, tiled=True),
        preferred_element_type=jnp.float32,
    )


def shards(dosage, pheno, perm, snp_weight):
    snp_rows = dosage.shape[0]
    sample_rows = dosage.shape[1]
    genes = pheno.shape[1]
    samp_count = lax.axis_size("samp")
    snp_count = lax.axis_size(SNP)
    total_samples = sample_rows * samp_count
    total_snps = snp_rows * snp_count
    null_count = perm.shape[0]
    copies = null_count + 1
    cols = genes // samp_count
    rows_here = genes // snp_count
    col_first = lax.axis_index("samp") * cols
    row_first = lax.axis_index(SNP) * rows_here
    dose = dosage.astype(jnp.float32)
    dose_half = dosage.astype(jnp.bfloat16)
    own_rows = lax.axis_index("samp") * sample_rows + jnp.arange(sample_rows)
    sources = jnp.concatenate([own_rows[None, :], perm], axis=0)
    piece = lax.all_gather(pheno, "samp", axis=0, tiled=True)
    targets = jnp.arange(piece.shape[0])
    picked = []
    for copy_index in range(copies):
        onehot = (sources[copy_index][:, None] == targets[None, :]).astype(jnp.bfloat16)
        picked.append(
            jnp.dot(dose_half, onehot, preferred_element_type=jnp.float32).astype(jnp.bfloat16)
        )
    stacked = jnp.concatenate(picked, axis=0)
    raw_scores = jnp.dot(stacked, piece, preferred_element_type=jnp.float32)
    dose_sum = jnp.sum(dose, axis=1)
    square_sum = jnp.sum(dose * dose, axis=1)
    pheno_sum = jnp.sum(pheno.astype(jnp.float32), axis=0)
    raw_scores = sent_and_summed(raw_scores, "samp", 1)
    dose_sum, square_sum, pheno_sum = together((dose_sum, square_sum, pheno_sum), "samp")
    pheno_part = lax.dynamic_slice_in_dim(pheno_sum, col_first, cols, 0)
    dose_mean = dose_sum / total_samples
    dose_square = square_sum / total_samples
    spread = jnp.sqrt(total_samples * (dose_square + 1e-05))
    mean_rows = jnp.tile(dose_mean, copies)[:, None]
    spread_rows = jnp.tile(spread, copies)[:, None]
    scores = ((raw_scores - mean_rows * pheno_part[None, :]) / spread_rows).astype(jnp.bfloat16)
    scores = gathered_copies(scores, "samp", 1)
    null_scores = scores[snp_rows:]
    weight_rows = jnp.tile(snp_weight, null_count)[:, None]
    weighted = (null_scores.astype(jnp.float32) * weight_rows).astype(jnp.bfloat16)
    right_part = lax.dynamic_slice_in_dim(null_scores, col_first, cols, 1)
    trace_value = over_copies(
        jnp.sum(weighted.astype(jnp.float32) * null_scores.astype(jnp.float32)), SNP
    ) / (null_count * total_snps)
    gram = summed_rows(
        lax.dot_general(
            weighted, right_part, (((0,), (0,)), ((), ())), preferred_element_type=jnp.float32
        ),
        SNP,
    ) / (null_count * total_snps)
    diagonal = (row_first + jnp.arange(rows_here))[:, None] == (col_first + jnp.arange(cols))[
        None, :
    ]
    identity = diagonal.astype(jnp.float32)
    scale = trace_value / genes + 1e-06
    scaled = gram / scale
    first_step = ((3.0 * identity - scaled) * 0.5).astype(jnp.bfloat16)
    first_image = product(scaled.astype(jnp.bfloat16), first_step).astype(jnp.bfloat16)
    second_prod = product(first_step, first_image)
    second_step = ((3.0 * identity - second_prod) * 0.5).astype(jnp.bfloat16)
    root_approx = product(second_step, first_step)
    root_block = (root_approx / jnp.sqrt(scale)).astype(jnp.bfloat16)
    white = jnp.dot(
        scores,
        lax.all_gather(root_block, SNP, axis=0, tiled=True),
        preferred_element_type=jnp.float32,
    )
    return white.astype(jnp.bfloat16).reshape(copies, snp_rows, cols)


def solution(mesh):
    finer = Mesh(
        mesh.devices.reshape(mesh.shape["samp"], 4, 8, 2), ("samp", "snp_0", "snp_1", "snp_2")
    )
    in_specs = (P(SNP, "samp"), P("samp", None), P(None, "samp"), P(SNP))
    out_specs = P(None, SNP, "samp")
    return jax.shard_map(
        shards, mesh=finer, in_specs=in_specs, out_specs=out_specs, check_vma=False
    )
```

profile of v0, /device:TPU:1, one launch (start us, length us, event | category | flops | bytes accessed | tf_op | source)
XLA Modules:
  0.0 671.6 jit_solution(3962241711823758204)
XLA Ops:
  6.5 0.7 all-gather.5.cloned.1.call-update
  7.3 1.0 multiply_reduce_fusion
  9.4 6.5 all-to-all-start.1
  15.9 0.9 fusion.21
  16.8 0.9 fusion.23
  17.8 0.9 fusion.25
  18.7 0.9 fusion.27
  19.7 0.9 fusion.29
  20.6 0.9 fusion.31
  21.5 0.9 fusion.33
  22.5 0.9 fusion.35
  23.4 0.9 fusion.37
  24.4 73.0 %all-gather.5.cloned.1.call-done = bf16[2048,2048]{1,0:T(8,128)(2,1)} async-done(((bf16[512,2048]{1,0:T(8,128)(2,1)}), bf16[2048,2048]{1,0:T(8,128)(2,1)}) %all-gather.5.cloned.1.call-update) | async-done | bytes 8388624 | tf_op jit(solution)/shard_map/all_gather | solution.py:84
  97.4 6.3 fusion.61
  103.7 2.2 copy.43
  106.5 3.7 all-to-all-start
  110.3 0.8 reduce_sum.67
  111.1 0.7 slice.53
  112.4 0.7 tile.6
  113.8 0.8 dynamic_slice.6
  114.5 35.0 %all-to-all-done = f32[4,432,512]{2,1,0:T(8,128)S(1)} async-done(((f32[4,432,512]{2,1,0:T(8,128)}), f32[4,432,512]{2,1,0:T(8,128)S(1)}, u32[]{:S(2)}, u32[]{:S(2)}) %all-to-all-start) | async-done | bytes 3538976 | tf_op jit(solution)/shard_map/all_to_all | solution.py:35
  149.5 1.4 reduce_sum.63
  150.9 1.4 divide_convert_fusion
  152.2 1.4 broadcast_in_dim.13
  153.6 4.5 all-to-all-start.2
  158.2 21.2 %all-to-all-done.2 = bf16[4,432,512]{2,1,0:T(8,128)(2,1)S(1)} async-done(((bf16[4,432,512]{2,1,0:T(8,128)(2,1)}), bf16[4,432,512]{2,1,0:T(8,128)(2,1)S(1)}, u32[]{:S(2)}, u32[]{:S(2)}) %all-to-all-start.2) | async-done | bytes 1769504 | tf_op jit(solution)/shard_map/all_to_all | solution.py:18
  179.5 2.3 copy.23
  181.8 2.3 slice.55
  184.1 3.3 fusion.47
  187.5 51.0 %reduce-scatter.4.cloned.1.call-done = f32[512,512]{1,0:T(8,128)} async-done(((f32[2048,512]{1,0:T(8,128)}), f32[512,512]{1,0:T(8,128)}) %reduce-scatter.4.cloned.1.call-update) | async-done | bytes 1048592 | tf_op jit(solution)/shard_map/reduce_scatter | solution.py:53
  238.5 36.1 %reduce-scatter.6.cloned.1.call-done = f32[64,512]{1,0:T(8,128)} async-done(((f32[512,512]{1,0:T(8,128)}), f32[64,512]{1,0:T(8,128)}) %reduce-scatter.6.cloned.1.call-update) | async-done | bytes 131088 | tf_op jit(solution)/shard_map/reduce_scatter | solution.py:53
  274.6 3.2 fusion.10
  277.8 1.3 broadcast_in_dim.14
  279.1 10.8 %all-to-all-start.3 = ((f32[64,1,1]{2,1,0:T(1,128)}), f32[64,1,1]{2,1,0:T(1,128)S(1)}, u32[]{:S(2)}, u32[]{:S(2)}) async-start(f32[64,1,1]{2,1,0:T(1,128)} %broadcast_in_dim.14), calls=%async_computation.6 | async-start | bytes 65536 | tf_op jit(solution)/shard_map/all_to_all | solution.py:18
  289.9 10.6 %all-to-all-done.3 = f32[64,1,1]{2,1,0:T(1,128)S(1)} async-done(((f32[64,1,1]{2,1,0:T(1,128)}), f32[64,1,1]{2,1,0:T(1,128)S(1)}, u32[]{:S(2)}, u32[]{:S(2)}) %all-to-all-start.3) | async-done | bytes 288 | tf_op jit(solution)/shard_map/all_to_all | solution.py:18
  301.9 1.5 fusion.55
  303.5 12.3 %all_to_all.37 = bf16[4,32,512]{2,1,0:T(8,128)(2,1)S(1)} all-to-all(bf16[4,32,512]{2,1,0:T(8,128)(2,1)S(1)} %broadcast_in_dim.16), channel_id=1, replica_groups=mesh['samp'=4,'snp_0'=4,'snp_1'=8,'snp_2'=2] {'samp'}, dimensions={0} | all-to-all | bytes 262144 | tf_op jit(solution)/shard_map/all_to_all | solution.py:18
  315.8 99.8 %all-gather.7.cloned.1.call-done = bf16[2048,512]{1,0:T(8,128)(2,1)} async-done(((bf16[32,512]{1,0:T(8,128)(2,1)}), bf16[2048,512]{1,0:T(8,128)(2,1)}) %all-gather.7.cloned.1.call-update) | async-done | bytes 2097168 | tf_op jit(solution)/shard_map/all_gather | solution.py:61
  415.6 2.7 convolution_convert_fusion.1
  418.4 10.1 %all_to_all.38 = bf16[4,32,512]{2,1,0:T(8,128)(2,1)S(1)} all-to-all(bf16[4,32,512]{2,1,0:T(8,128)(2,1)S(1)} %broadcast_in_dim.15), channel_id=1, replica_groups=mesh['samp'=4,'snp_0'=4,'snp_1'=8,'snp_2'=2] {'samp'}, dimensions={0} | all-to-all | bytes 262144 | tf_op jit(solution)/shard_map/all_to_all | solution.py:18
  428.5 105.5 %all-gather.9.cloned.1.call-done = bf16[2048,512]{1,0:T(8,128)(2,1)} async-done(((bf16[32,512]{1,0:T(8,128)(2,1)}), bf16[2048,512]{1,0:T(8,128)(2,1)}) %all-gather.9.cloned.1.call-update) | async-done | bytes 2097168 | tf_op jit(solution)/shard_map/all_gather | solution.py:61
  534.0 2.0 fusion.50
  536.1 0.7 broadcast_in_dim.17
  536.8 7.5 %all-to-all-start.6 = ((bf16[4,32,512]{2,1,0:T(8,128)(2,1)}), bf16[4,32,512]{2,1,0:T(8,128)(2,1)S(1)}, u32[]{:S(2)}, u32[]{:S(2)}) async-start(bf16[4,32,512]{2,1,0:T(8,128)(2,1)} %broadcast_in_dim.17), calls=%async_computation.9 | async-start | bytes 262144 | tf_op jit(solution)/shard_map/all_to_all | solution.py:18
  544.3 3.5 all-to-all-done.6
  547.8 2.7 fusion.51
  550.8 110.5 %all-gather.11.cloned.1.call-done = bf16[2048,512]{1,0:T(8,128)(2,1)} async-done(((bf16[32,512]{1,0:T(8,128)(2,1)}), bf16[2048,512]{1,0:T(8,128)(2,1)}) %all-gather.11.cloned.1.call-update) | async-done | bytes 2097168 | tf_op jit(solution)/shard_map/all_gather | solution.py:134
  661.3 3.4 convolution_convert_fusion
  (49 shorter events, 4.4 us)
Async XLA Ops:
  6.5 1.7 copy-start
  6.5 9.3 %copy-start.1 = (s32[48,512]{1,0:T(8,128)S(1)}, s32[48,512]{1,0:T(8,128)}, u32[]{:S(2)}) copy-start(s32[48,512]{1,0:T(8,128)} %param.4) | copy-start | bytes 294916
  6.5 9.3 %copy-start.4 = (s32[8,512]{1,0:T(8,128)S(1)}, s32[8,512]{1,0:T(8,128)}, u32[]{:S(2)}) copy-start(s32[8,512]{1,0:T(8,128)} %param.6) | copy-start | bytes 49156
  6.5 90.9 %all-gather.5.cloned.1.call-start = ((), (), s32[]{:S(2)}) async-start(), calls=%async_computation.10 | async-start | bytes 10485760 | tf_op jit(solution)/shard_map/all_gather | solution.py:84
  9.4 96.5 %all-to-all-start.1 = ((f32[4,1,2144]{2,1,0:T(1,128)}), f32[4,1,2144]{2,1,0:T(1,128)S(1)}, u32[]{:S(2)}, u32[]{:S(2)}) async-start(f32[4,1,2144]{2,1,0:T(1,128)} %broadcast_in_dim.12), calls=%async_computation.1 | async-start | bytes 69632 | tf_op jit(solution)/shard_map/all_to_all | solution.py:18
  105.9 0.6 copy-start.3
  106.5 43.0 %all-to-all-start = ((f32[4,432,512]{2,1,0:T(8,128)}), f32[4,432,512]{2,1,0:T(8,128)S(1)}, u32[]{:S(2)}, u32[]{:S(2)}) async-start(f32[4,432,512]{2,1,0:T(8,128)} %bitcast.84), calls=%async_computation | async-start | bytes 7077888 | tf_op jit(solution)/shard_map/all_to_all | solution.py:35
  114.5 36.3 %copy-start.5 = (f32[432]{0:T(512)S(1)}, f32[432]{0:T(512)}, u32[]{:S(2)}) copy-start(f32[432]{0:T(512)} %mul.69) | copy-start | bytes 5188
  153.6 4.6 copy-start.6
  153.6 25.9 %all-to-all-start.2 = ((bf16[4,432,512]{2,1,0:T(8,128)(2,1)}), bf16[4,432,512]{2,1,0:T(8,128)(2,1)S(1)}, u32[]{:S(2)}, u32[]{:S(2)}) async-start(bf16[4,432,512]{2,1,0:T(8,128)(2,1)} %broadcast_in_dim.13), calls=%async_computation.2 | async-start | bytes 3538944 | tf_op jit(solution)/shard_map/all_to_all | solution.py:18
  158.1 80.3 %reduce-scatter.4.cloned.1.call-start = ((), (), s32[]{:S(2)}) async-start(), calls=%async_computation.11 | async-start | bytes 5242880 | tf_op jit(solution)/shard_map/reduce_scatter | solution.py:53
  187.4 87.2 %reduce-scatter.6.cloned.1.call-start = ((), (), s32[]{:S(2)}) async-start(), calls=%async_computation.12 | async-start | bytes 1179648 | tf_op jit(solution)/shard_map/reduce_scatter | solution.py:53
  238.5 63.4 %reduce-scatter.8.cloned.1.call-start = ((), (), s32[]{:S(2)}) async-start(), calls=%async_computation.13 | async-start | bytes 196608 | tf_op jit(solution)/shard_map/reduce_scatter | solution.py:53
  279.1 21.4 %all-to-all-start.3 = ((f32[64,1,1]{2,1,0:T(1,128)}), f32[64,1,1]{2,1,0:T(1,128)S(1)}, u32[]{:S(2)}, u32[]{:S(2)}) async-start(f32[64,1,1]{2,1,0:T(1,128)} %broadcast_in_dim.14), calls=%async_computation.6 | async-start | bytes 65536 | tf_op jit(solution)/shard_map/all_to_all | solution.py:18
  289.9 125.8 %all-gather.7.cloned.1.call-start = ((), (), s32[]{:S(2)}) async-start(), calls=%async_computation.14 | async-start | bytes 2129920 | tf_op jit(solution)/shard_map/all_gather | solution.py:61
  303.4 114.9 %copy-start.2 = (bf16[32,512]{1,0:T(8,128)(2,1)S(1)}, bf16[32,512]{1,0:T(8,128)(2,1)}, u32[]{:S(2)}) copy-start(bf16[32,512]{1,0:T(8,128)(2,1)} %get-tuple-element.8) | copy-start | bytes 98308
  303.4 230.6 %all-gather.9.cloned.1.call-start = ((), (), s32[]{:S(2)}) async-start(), calls=%async_computation.15 | async-start | bytes 2129920 | tf_op jit(solution)/shard_map/all_gather | solution.py:61
  536.8 11.1 %all-to-all-start.6 = ((bf16[4,32,512]{2,1,0:T(8,128)(2,1)}), bf16[4,32,512]{2,1,0:T(8,128)(2,1)S(1)}, u32[]{:S(2)}, u32[]{:S(2)}) async-start(bf16[4,32,512]{2,1,0:T(8,128)(2,1)} %broadcast_in_dim.17), calls=%async_computation.9 | async-start | bytes 262144 | tf_op jit(solution)/shard_map/all_to_all | solution.py:18
  544.2 117.1 %all-gather.11.cloned.1.call-start = ((), (), s32[]{:S(2)}) async-start(), calls=%async_computation.16 | async-start | bytes 2129920 | tf_op jit(solution)/shard_map/all_gather | solution.py:134
Sparse Core Ops, SparseCore 0:
  9.2 88.1 all-gather.4
  187.5 50.8 reduce-scatter.3
  241.1 33.4 reduce-scatter.5
  277.1 20.5 reduce-scatter.7
  303.6 112.0 all-gather.6
  419.7 114.3 all-gather.8
  550.6 110.6 all-gather.10
where the time goes:
time: 675 us; the launch traced here: 672 us
  waiting for transfers between devices  547 us (81%)
  starting transfers between devices  33.2 us (5%)
  matrix products  28.7 us (4%)
  blocking collectives  22.4 us (3%)
  local copies, waits for them, and re-layouts  14.8 us (2%)
  between operations  14.4 us (2%)
  other arithmetic  10.9 us (2%)
    all_gather x2, waiting for transfers between devices, product(): lax.all_gather(right_block, SNP, axis=0, tiled=True)  205 us
    all_gather x1, waiting for transfers between devices, shards(): lax.all_gather(root_block, SNP, axis=0, tiled=True)  111 us
    reduce_scatter x3, waiting for transfers between devices, summed_rows(): so_far = lax.psum_scatter(so_far, axis, scatter_dimension=0, tiled=True)  87.1 us
    all_gather x1, waiting for transfers between devices, shards(): piece = lax.all_gather(pheno, 'samp', axis=0, tiled=True)  73 us
    all_to_all x4, waiting for transfers between devices, copy_for_each(): lax.all_to_all(jnp.broadcast_to(array[None], (devices, *array.shape)), ax...  35.4 us
    all_to_all x1, waiting for transfers between devices, sent_and_summed(): lax.all_to_all(parts, axis, split_axis=0, concat_axis=0, tiled=True)  35 us
    all_to_all x4, starting transfers between devices, copy_for_each(): lax.all_to_all(jnp.broadcast_to(array[None], (devices, *array.shape)), ax...  29.3 us
    all_to_all x2, blocking collectives, copy_for_each(): lax.all_to_all(jnp.broadcast_to(array[None], (devices, *array.shape)), ax...  22.4 us
  transfers between devices with their start and end apart: 12, of which 10 were waited for; matrix products, arithmetic and copies ran while one was open for 4% of the time, Pallas kernels for 0%

commit v1 on v0

v1 whole, which is shorter than its diff:
```python
import jax
import jax.numpy as jnp
from jax import lax
from jax.sharding import Mesh
from jax.sharding import PartitionSpec as P

SAMP = ("y_lo", "core")
SNP = ("x", "z", "y_hi")
F32 = jnp.float32
BF16 = jnp.bfloat16
NT = (((1,), (1,)), ((), ()))
LOW = 256


def sent_parts(array, axis):
    return lax.all_to_all(array, axis, split_axis=0, concat_axis=0, tiled=True)


def copies_from(array, axis):
    devices = lax.axis_size(axis)
    return sent_parts(jnp.broadcast_to(array[None], (devices, *array.shape)), axis)


def summed_share(array, axis):
    devices = lax.axis_size(axis)
    rows = array.shape[0] // devices
    arrived = sent_parts(array.astype(BF16).reshape(devices, rows, array.shape[1]), axis)
    return jnp.sum(arrived.astype(F32), axis=0)


def gathered_rows(array, axis):
    got = copies_from(array, axis)
    return got.reshape(got.shape[0] * got.shape[1], got.shape[2])


def shards(dosage, pheno, perm, snp_weight):
    snps, own = dosage.shape
    genes = pheno.shape[1]
    groups = lax.axis_size(SAMP)
    samples = own * groups
    total_snps = snps * lax.axis_size(SNP)
    nulls = perm.shape[0]
    copies = nulls + 1
    rows = copies * snps
    cols = genes // groups
    me = lax.axis_index(SAMP)
    coded = jnp.concatenate(
        [dosage, perm // LOW, perm % LOW], axis=0
    ).astype(BF16)
    coded = copies_from(coded, SAMP)
    coded = jnp.moveaxis(coded, 0, 1).reshape(coded.shape[1], samples)
    pheno_parts = jnp.moveaxis(pheno.reshape(own, groups, cols), 1, 0)
    pheno_cols = sent_parts(pheno_parts, SAMP).reshape(samples, cols)
    dose = coded[:snps]
    high = coded[snps : snps + nulls]
    low = coded[snps + nulls :]
    steps = samples // LOW
    step_ids = jnp.arange(steps).astype(BF16)[:, None, None]
    low_ids = jnp.arange(LOW).astype(BF16)[:, None]
    placed = [dose]
    for k in range(nulls):
        masked = jnp.where(high[k][None, None, :] == step_ids, dose[None], jnp.zeros((), BF16))
        onehot = (low[k][None, :] == low_ids).astype(BF16)
        part = lax.dot_general(
            masked.reshape(steps * snps, samples), onehot, NT, preferred_element_type=F32
        ).astype(BF16)
        part = part.reshape(steps, snps, LOW)
        placed.append(jnp.concatenate([part[h] for h in range(steps)], axis=1))
    placed = jnp.concatenate(placed, axis=0)
    raw = jnp.dot(placed, pheno_cols, preferred_element_type=F32)
    dose32 = dose.astype(F32)
    dose_mean = jnp.sum(dose32, axis=1) / samples
    dose_square = jnp.sum(dose32 * dose32, axis=1) / samples
    pheno_sum = jnp.sum(pheno_cols.astype(F32), axis=0)
    spread = jnp.sqrt(samples * (dose_square + 1e-05))
    mean_rows = jnp.tile(dose_mean, copies)[:, None]
    spread_rows = jnp.tile(spread, copies)[:, None]
    scores = ((raw - mean_rows * pheno_sum[None, :]) / spread_rows).astype(BF16)
    every = copies_from(scores, SAMP)
    every = jnp.moveaxis(every, 0, 1).reshape(rows, genes)
    weight_rows = jnp.tile(snp_weight, nulls)[:, None]
    weighted = (every[snps:].astype(F32) * weight_rows).astype(BF16)
    gram = lax.dot_general(
        weighted, scores[snps:], (((0,), (0,)), ((), ())), preferred_element_type=F32
    )
    for axis in ("x", "y_hi", "z"):
        gram = summed_share(gram, axis)
    gram = (gram / (nulls * total_snps)).astype(BF16)
    for axis in ("z", "y_hi", "x"):
        gram = gathered_rows(gram, axis)
    gram = copies_from(gram, SAMP)
    trace_value = F32(0)
    for a in range(groups):
        block = gram[a, a * cols : (a + 1) * cols].astype(F32)
        trace_value += jnp.sum(jnp.where(jnp.eye(cols, dtype=bool), block, F32(0)))
    scale = trace_value / genes + 1e-06

    def image(left):
        left = left.astype(BF16)
        parts = [jnp.dot(left, gram[a], preferred_element_type=F32) for a in range(groups)]
        return jnp.concatenate(parts, axis=1) / scale

    def step(left):
        return 1.5 * left - 0.5 * image(left)

    share = rows // groups
    mine = lax.dynamic_slice_in_dim(every, me * share, share, 0).astype(F32)
    inner = step(image(step(mine)))
    white = step(1.5 * mine - 0.5 * inner) / jnp.sqrt(scale)
    white = white.astype(BF16).reshape(share, groups, cols)
    white = sent_parts(jnp.moveaxis(white, 1, 0), SAMP)
    return white.reshape(copies, snps, cols)


def solution(mesh):
    finer = Mesh(mesh.devices.reshape(2, 2, 4, 8, 2), (*SAMP, *SNP))
    in_specs = (P(SNP, SAMP), P(SAMP, None), P(None, SAMP), P(SNP))
    return jax.shard_map(
        shards, mesh=finer, in_specs=in_specs, out_specs=P(None, SNP, SAMP), check_vma=False
    )
```

time: 675 us -> 371 us (0.55)
  waiting for transfers between devices: 547 us -> 113 us
  blocking collectives: 22.4 us -> 109 us
  local copies, waits for them, and re-layouts: 14.8 us -> 61.6 us
  matrix products: 28.7 us -> 43.9 us
  between operations: 14.4 us -> 2.87 us
    all_gather x4 -> x0, waiting for transfers between devices: 389 us -> none  [the longest x2 205 us: product(): lax.all_gather(right_block, SNP, axis=0, tiled=True)]
    reduce_scatter x3 -> x0, waiting for transfers between devices: 87.1 us -> none  [summed_rows(): so_far = lax.psum_scatter(so_far, axis, scatter_dimension=0, tiled=True)]
    all_to_all x2 -> x7, blocking collectives: 22.4 us -> 109 us  [sent_parts(): return lax.all_to_all(array, axis, split_axis=0, concat_axis=0, tiled=True)]
    unnamed x14 -> x88, local copies, waits for them, and re-layouts: 0.64 us -> 44.5 us
    all_to_all x5 -> x4, waiting for transfers between devices: 70.3 us -> 113 us  [sent_parts(): return lax.all_to_all(array, axis, split_axis=0, concat_axis=0, tiled=True)]
    dot_general x15 -> x26, matrix products: 28.7 us -> 43.9 us  [the longest x16 32.9 us: image(): jnp.dot(left, gram[a], preferred_element_type=F32)]
    all_to_all x5 -> x4, starting transfers between devices: 33 us -> 28.6 us  [sent_parts(): return lax.all_to_all(array, axis, split_axis=0, concat_axis=0, tiled=True)]
  transfers between devices with their start and end apart: 12 -> 4, of which waited for: 10 -> 3; matrix products, arithmetic and copies ran while one was open for 4% -> 15% of each run, Pallas kernels for 0% -> 0%
where the time goes in v1:
time: 371 us; the launch traced here: 369 us
  waiting for transfers between devices  113 us (30%)
  blocking collectives  109 us (29%)
  local copies, waits for them, and re-layouts  61.6 us (17%)
  matrix products  43.9 us (12%)
  starting transfers between devices  28.6 us (8%)
  other arithmetic  9.98 us (3%)
    all_to_all x4, waiting for transfers between devices, sent_parts(): return lax.all_to_all(array, axis, split_axis=0, concat_axis=0, tiled=True)  113 us
    all_to_all x7, blocking collectives, sent_parts(): return lax.all_to_all(array, axis, split_axis=0, concat_axis=0, tiled=True)  109 us
    unnamed x88, local copies, waits for them, and re-layouts  44.5 us
    dot_general x16, matrix products, image(): jnp.dot(left, gram[a], preferred_element_type=F32)  32.9 us
    all_to_all x4, starting transfers between devices, sent_parts(): return lax.all_to_all(array, axis, split_axis=0, concat_axis=0, tiled=True)  28.6 us
  transfers between devices with their start and end apart: 4, of which 3 were waited for; matrix products, arithmetic and copies ran while one was open for 15% of the time, Pallas kernels for 0%

profile of v1, /device:TPU:1, one launch (start us, length us, event | category | flops | bytes accessed | tf_op | source)
XLA Modules:
  0.0 369.4 jit_solution(3144948970478126532)
XLA Ops:
  0.0 0.7 fusion.98
  0.7 0.9 convert.16
  1.7 0.7 broadcast_in_dim.140
  2.4 6.6 %all-to-all-start = ((bf16[4,64,512]{2,1,0:T(8,128)(2,1)}), bf16[4,64,512]{2,1,0:T(8,128)(2,1)S(1)}, u32[]{:S(2)}, u32[]{:S(2)}) async-start(bf16[4,64,512]{2,1,0:T(8,128)(2,1)} %broadcast_in_dim.140), calls=%async_computation | async-start | bytes 524288 | tf_op jit(solution)/shard_map/all_to_all | solution.py:16
  9.0 3.9 %copy.22 = bf16[512,2048]{0,1:T(8,128)(2,1)} copy(bf16[512,2048]{1,0:T(8,128)(2,1)} %param.5) | data formatting | bytes 4194304 | tf_op args[1]
  12.9 1.2 all-to-all-done
  14.2 4.4 %all-to-all-start.1 = ((bf16[4,512,512]{1,2,0:T(8,128)(2,1)}), bf16[4,512,512]{1,2,0:T(8,128)(2,1)S(1)}, u32[]{:S(2)}, u32[]{:S(2)}) async-start(bf16[4,512,512]{1,2,0:T(8,128)(2,1)} %bitcast.127), calls=%async_computation.1 | async-start | bytes 4194304 | tf_op jit(solution)/shard_map/all_to_all | solution.py:16
  20.1 2.3 broadcast_select_fusion
  61.9 2.1 fusion.58
  69.0 2.4 copy.23
  71.7 1.2 copy-done.1
  73.0 2.6 fusion.36
  75.5 1.4 broadcast_in_dim.151
  76.9 3.7 %all-to-all-start.2 = ((bf16[4,432,512]{2,1,0:T(8,128)(2,1)}), bf16[4,432,512]{2,1,0:T(8,128)(2,1)S(1)}, u32[]{:S(2)}, u32[]{:S(2)}) async-start(bf16[4,432,512]{2,1,0:T(8,128)(2,1)} %broadcast_in_dim.151), calls=%async_computation.2 | async-start | bytes 3538944 | tf_op jit(solution)/shard_map/all_to_all | solution.py:16
  80.7 21.2 %all-to-all-done.2 = bf16[4,432,512]{2,1,0:T(8,128)(2,1)S(1)} async-done(((bf16[4,432,512]{2,1,0:T(8,128)(2,1)}), bf16[4,432,512]{2,1,0:T(8,128)(2,1)S(1)}, u32[]{:S(2)}, u32[]{:S(2)}) %all-to-all-start.2) | async-done | bytes 1769504 | tf_op jit(solution)/shard_map/all_to_all | solution.py:16
  102.0 2.4 copy.24
  104.3 2.3 slice.562
  106.6 1.2 convolution_convert_fusion
  107.9 28.7 %all_to_all.55 = bf16[4,512,512]{2,1,0:T(8,128)(2,1)} all-to-all(bf16[4,512,512]{2,1,0:T(8,128)(2,1)S(1)} %bitcast.140), channel_id=1, replica_groups=mesh['y_lo'=2,'core'=2,'x'=4,'z'=8,'y_hi'=2] {'x'}, dimensions={0} | all-to-all | bytes 4194304 | tf_op jit(solution)/shard_map/all_to_all | solution.py:16
  136.6 2.2 reduce_sum.99
  138.8 9.6 %all_to_all.56 = bf16[2,256,512]{2,1,0:T(8,128)(2,1)S(1)} all-to-all(bf16[2,256,512]{2,1,0:T(8,128)(2,1)S(1)} %bitcast.141), channel_id=1, replica_groups=mesh['y_lo'=2,'core'=2,'x'=4,'z'=8,'y_hi'=2] {'y_hi'}, dimensions={0} | all-to-all | bytes 1048576 | tf_op jit(solution)/shard_map/all_to_all | solution.py:16
  148.5 17.5 %all_to_all.57 = bf16[8,32,512]{2,1,0:T(8,128)(2,1)S(1)} all-to-all(bf16[8,32,512]{2,1,0:T(8,128)(2,1)S(1)} %bitcast.155), channel_id=1, replica_groups=mesh['y_lo'=2,'core'=2,'x'=4,'z'=8,'y_hi'=2] {'z'}, dimensions={0} | all-to-all | bytes 524288 | tf_op jit(solution)/shard_map/all_to_all | solution.py:16
  166.0 11.8 %all_to_all.58 = bf16[8,32,512]{2,1,0:T(8,128)(2,1)S(1)} all-to-all(bf16[8,32,512]{2,1,0:T(8,128)(2,1)S(1)} %broadcast_in_dim.152), channel_id=1, replica_groups=mesh['y_lo'=2,'core'=2,'x'=4,'z'=8,'y_hi'=2] {'z'}, dimensions={0} | all-to-all | bytes 524288 | tf_op jit(solution)/shard_map/all_to_all | solution.py:16
  177.9 9.3 %all_to_all.59 = bf16[2,256,512]{2,1,0:T(8,128)(2,1)S(1)} all-to-all(bf16[2,256,512]{2,1,0:T(8,128)(2,1)S(1)} %broadcast_in_dim.154), channel_id=1, replica_groups=mesh['y_lo'=2,'core'=2,'x'=4,'z'=8,'y_hi'=2] {'y_hi'}, dimensions={0} | all-to-all | bytes 1048576 | tf_op jit(solution)/shard_map/all_to_all | solution.py:16
  187.4 21.6 %all_to_all.60 = bf16[4,512,512]{2,1,0:T(8,128)(2,1)S(1)} all-to-all(bf16[4,512,512]{2,1,0:T(8,128)(2,1)S(1)} %broadcast_in_dim.156), channel_id=1, replica_groups=mesh['y_lo'=2,'core'=2,'x'=4,'z'=8,'y_hi'=2] {'x'}, dimensions={0} | all-to-all | bytes 4194304 | tf_op jit(solution)/shard_map/all_to_all | solution.py:16
  209.0 3.9 %broadcast_in_dim.158 = bf16[4,2048,512]{2,1,0:T(8,128)(2,1)} broadcast(bf16[2048,512]{1,0:T(8,128)(2,1)S(1)} %bitcast.126), dimensions={1,2} | broadcast | bytes 10485760 | tf_op jit(solution)/shard_map/broadcast_in_dim | solution.py:21
  212.8 13.8 %all-to-all-start.9 = ((bf16[4,2048,512]{2,1,0:T(8,128)(2,1)}), bf16[4,2048,512]{2,1,0:T(8,128)(2,1)}, u32[]{:S(2)}, u32[]{:S(2)}) async-start(bf16[4,2048,512]{2,1,0:T(8,128)(2,1)} %broadcast_in_dim.158), calls=%async_computation.9 | async-start | bytes 16777216 | tf_op jit(solution)/shard_map/all_to_all | solution.py:16
  226.6 1.5 copy.29
  228.1 90.9 %all-to-all-done.9 = bf16[4,2048,512]{2,1,0:T(8,128)(2,1)} async-done(((bf16[4,2048,512]{2,1,0:T(8,128)(2,1)}), bf16[4,2048,512]{2,1,0:T(8,128)(2,1)}, u32[]{:S(2)}, u32[]{:S(2)}) %all-to-all-start.9) | async-done | bytes 8388640 | tf_op jit(solution)/shard_map/all_to_all | solution.py:16
  319.0 2.3 fusion.61
  323.7 2.0 fusion.22
  325.8 2.0 fusion.26
  327.8 2.0 fusion.30
  329.9 2.0 fusion.34
  332.2 2.1 fusion.21
  334.2 2.1 fusion.25
  336.3 2.1 fusion.29
  338.4 2.1 fusion.33
  340.4 2.1 fusion.20
  342.5 2.1 fusion.24
  344.6 2.1 fusion.28
  346.7 2.1 fusion.32
  349.1 2.1 fusion.19
  351.2 2.1 fusion.23
  353.3 2.1 fusion.27
  355.3 2.1 fusion.31
  357.9 10.7 %all_to_all.61 = bf16[4,108,512]{2,1,0:T(8,128)(2,1)S(1)} all-to-all(bf16[4,108,512]{2,1,0:T(8,128)(2,1)S(1)} %bitcast.142), channel_id=1, replica_groups=mesh['y_lo'=2,'core'=2,'x'=4,'z'=8,'y_hi'=2] {'y_lo','core'}, dimensions={0} | all-to-all | bytes 884736 | tf_op jit(solution)/shard_map/all_to_all | solution.py:16
  368.6 0.8 reshape.550
  (121 shorter events, 47.7 us)
Async XLA Ops:
  2.4 11.8 %all-to-all-start = ((bf16[4,64,512]{2,1,0:T(8,128)(2,1)}), bf16[4,64,512]{2,1,0:T(8,128)(2,1)S(1)}, u32[]{:S(2)}, u32[]{:S(2)}) async-start(bf16[4,64,512]{2,1,0:T(8,128)(2,1)} %broadcast_in_dim.140), calls=%async_computation | async-start | bytes 524288 | tf_op jit(solution)/shard_map/all_to_all | solution.py:16
  14.2 54.8 %all-to-all-start.1 = ((bf16[4,512,512]{1,2,0:T(8,128)(2,1)}), bf16[4,512,512]{1,2,0:T(8,128)(2,1)S(1)}, u32[]{:S(2)}, u32[]{:S(2)}) async-start(bf16[4,512,512]{1,2,0:T(8,128)(2,1)} %bitcast.127), calls=%async_computation.1 | async-start | bytes 4194304 | tf_op jit(solution)/shard_map/all_to_all | solution.py:16
  71.4 1.6 copy-start.1
  76.9 3.7 %copy-start.2 = (f32[48]{0:T(128)S(1)}, f32[48]{0:T(128)}, u32[]{:S(2)}) copy-start(f32[48]{0:T(128)} %param.7) | copy-start | bytes 580
  76.9 25.0 %all-to-all-start.2 = ((bf16[4,432,512]{2,1,0:T(8,128)(2,1)}), bf16[4,432,512]{2,1,0:T(8,128)(2,1)S(1)}, u32[]{:S(2)}, u32[]{:S(2)}) async-start(bf16[4,432,512]{2,1,0:T(8,128)(2,1)} %broadcast_in_dim.151), calls=%async_computation.2 | async-start | bytes 3538944 | tf_op jit(solution)/shard_map/all_to_all | solution.py:16
  212.8 106.2 %all-to-all-start.9 = ((bf16[4,2048,512]{2,1,0:T(8,128)(2,1)}), bf16[4,2048,512]{2,1,0:T(8,128)(2,1)}, u32[]{:S(2)}, u32[]{:S(2)}) async-start(bf16[4,2048,512]{2,1,0:T(8,128)(2,1)} %broadcast_in_dim.158), calls=%async_computation.9 | async-start | bytes 16777216 | tf_op jit(solution)/shard_map/all_to_all | solution.py:16
  228.1 95.6 %copy-start = (bf16[4,54,8,512]{3,2,0,1:T(8,128)(2,1)S(1)}, bf16[4,54,8,512]{3,2,0,1:T(8,128)(2,1)}, u32[]{:S(2)}) copy-start(bf16[4,54,8,512]{3,2,0,1:T(8,128)(2,1)} %copy.29) | copy-start | bytes 5308420

commit v2 on v1

v2 whole, which is shorter than its diff:
```python
import functools

import jax
import jax.numpy as jnp
from jax import lax
from jax.experimental import pallas as pl
from jax.experimental.pallas import tpu as pltpu
from jax.sharding import Mesh
from jax.sharding import PartitionSpec as P

SAMP = ("y_lo", "core")
SNP = ("x", "z", "y_hi")
F32 = jnp.float32
BF16 = jnp.bfloat16
NT = (((1,), (1,)), ((), ()))
TN = (((0,), (0,)), ((), ()))
LOW = 256
MESH = pl.DeviceIdType.MESH
LANES = 128


def sent_parts(array, axis):
    return lax.all_to_all(array, axis, split_axis=0, concat_axis=0, tiled=True)


def copies_from(array, axis):
    devices = lax.axis_size(axis)
    return sent_parts(jnp.broadcast_to(array[None], (devices, *array.shape)), axis)


def spread_kernel(
    total, part, out, x_slots, pair, acc, slots, chunk,
    x_send, x_recv, r_send, r_recv, g_send, g_recv,
    xg_send, xg_recv, y_send, y_recv, c_send, c_recv, own_sem,
):
    rows, cols = part.shape
    block, half, bit = rows // 4, rows // 8, rows // 64
    x, z, y_hi = lax.axis_index("x"), lax.axis_index("z"), lax.axis_index("y_hi")
    y_lo, core = lax.axis_index("y_lo"), lax.axis_index("core")
    right, left, across = lax.rem(x + 1, 4), lax.rem(x + 3, 4), lax.rem(x + 2, 4)
    to_right, to_left = {"x": right}, {"x": left}
    sibling = {"core": 1 - core}
    near, far = {"y_lo": 1 - y_lo}, {"y_lo": 1 - y_lo, "y_hi": 1 - y_hi}
    peers = [(dz, dy) for dz in range(8) for dy in range(2) if dz or dy]

    def peer(dz, dy):
        there = {"z": lax.rem(z + dz, 8)}
        if dy:
            there["y_hi"] = 1 - y_hi
        return there

    barrier = pltpu.get_barrier_semaphore()
    greeted = [to_right, to_left, sibling, near, far] + [peer(*p) for p in peers]
    for there in greeted:
        pl.semaphore_signal(barrier, inc=1, device_id=there, device_id_type=MESH)
    pl.semaphore_wait(barrier, len(greeted))

    started = []

    def send(src, dst, send_sem, recv_sem, there):
        copy = pltpu.make_async_remote_copy(
            src_ref=src, dst_ref=dst, send_sem=send_sem, recv_sem=recv_sem,
            device_id=there, device_id_type=MESH,
        )
        copy.start()
        started.append(copy)
        return copy

    def half_of(owner, h):
        return part.at[pl.ds(pl.multiple_of(owner * block + h * half, half), half)]

    def x_sent(i, src, there):
        return send(src, x_slots.at[i], x_send.at[i], x_recv.at[i], there)

    hop_r = x_sent(0, half_of(across, 0), to_right)
    hop_l = x_sent(1, half_of(across, 1), to_left)
    own_r = x_sent(2, half_of(right, 1), to_right)
    own_l = x_sent(3, half_of(left, 0), to_left)

    def added(dst, sources):
        @pl.loop(0, half, step=32)
        def _(r):
            at = pl.ds(pl.multiple_of(r, 32), 32)
            value = sources[0][at, :].astype(F32)
            for source in sources[1:]:
                value += source[at, :].astype(F32)
            dst[at, :] = value.astype(BF16)

    hop_r.wait_recv()
    added(pair.at[0], [half_of(right, 0), x_slots.at[0]])
    sum_r = x_sent(4, pair.at[0], to_right)
    hop_l.wait_recv()
    added(pair.at[1], [half_of(left, 1), x_slots.at[1]])
    sum_l = x_sent(5, pair.at[1], to_left)
    own_l.wait_recv()
    sum_r.wait_recv()
    added(acc.at[pl.ds(0, half)], [half_of(x, 0), x_slots.at[3], x_slots.at[4]])
    own_r.wait_recv()
    sum_l.wait_recv()
    added(acc.at[pl.ds(half, half)], [half_of(x, 1), x_slots.at[2], x_slots.at[5]])

    def bit_at(at_y, at_z):
        return pl.ds(pl.multiple_of((at_y * 8 + at_z) * bit, bit), bit)

    arrive = []
    for i, (dz, dy) in enumerate(peers):
        at_y = 1 - y_hi if dy else y_hi
        arrive.append(
            send(
                acc.at[bit_at(at_y, lax.rem(z + dz, 8))], slots.at[i],
                r_send.at[i], r_recv.at[i], peer(dz, dy),
            )
        )
    value = acc[bit_at(y_hi, z), :].astype(F32)
    for i, copy in enumerate(arrive):
        copy.wait_recv()
        value += slots[i].astype(F32)
    chunk[...] = (value / total).astype(BF16)

    piece = y_lo * 2 + core
    mine = pl.ds(pl.multiple_of(x * block + (y_hi * 8 + z) * bit, bit), bit)
    stay = pltpu.make_async_copy(chunk, out.at[piece, mine], own_sem)
    stay.start()
    arrive = []
    for i, (dz, dy) in enumerate(peers):
        arrive.append(
            send(chunk, out.at[piece, mine], g_send.at[i], g_recv.at[i], peer(dz, dy))
        )
    stay.wait()
    for copy in arrive:
        copy.wait_recv()

    def at_half(which, owner, h):
        return out.at[which, pl.ds(pl.multiple_of(owner * block + h * half, half), half)]

    def at_block(which, owner):
        return out.at[which, pl.ds(pl.multiple_of(owner * block, block), block)]

    def passed(src, sems, i, there):
        return send(src, src, sems[0].at[i], sems[1].at[i], there)

    xs, ys, cs = (xg_send, xg_recv), (y_send, y_recv), (c_send, c_recv)

    def to_y(i, owner):
        return (
            passed(at_half(piece, owner, 0), ys, 2 * i, near),
            passed(at_half(piece, owner, 1), ys, 2 * i + 1, far),
        )

    go_r = passed(at_block(piece, x), xs, 0, to_right)
    go_l = passed(at_block(piece, x), xs, 1, to_left)
    y_own = to_y(0, x)
    c_all = [passed(at_block(piece, x), cs, 0, sibling)]
    go_r.wait_recv()
    hop_r = passed(at_half(piece, left, 0), xs, 2, to_right)
    y_left = to_y(1, left)
    go_l.wait_recv()
    hop_l = passed(at_half(piece, right, 1), xs, 3, to_left)
    y_right = to_y(2, right)
    c_all.append(passed(at_block(piece, left), cs, 1, sibling))
    c_all.append(passed(at_block(piece, right), cs, 2, sibling))
    other = (1 - y_lo) * 2 + core

    def from_y(copies, owner, i):
        for h, copy in enumerate(copies):
            copy.wait_recv()
        c_all.append(passed(at_block(other, owner), cs, i, sibling))

    from_y(y_own, x, 3)
    hop_r.wait_recv()
    y_far = [passed(at_half(piece, across, 0), ys, 6, near)]
    hop_l.wait_recv()
    y_far.append(passed(at_half(piece, across, 1), ys, 7, far))
    c_all.append(passed(at_block(piece, across), cs, 4, sibling))
    from_y(y_left, left, 5)
    from_y(y_right, right, 6)
    from_y(y_far, across, 7)
    for copy in c_all:
        copy.wait_recv()
    for copy in started:
        copy.wait_send()


def spread(part, total):
    rows, cols = part.shape
    dma = pltpu.SemaphoreType.DMA
    pairs = [6, 6, 15, 15, 15, 15, 4, 4, 8, 8, 8, 8]
    return pl.pallas_call(
        functools.partial(spread_kernel, total),
        out_shape=jax.ShapeDtypeStruct((4, rows, cols), BF16),
        in_specs=[pl.BlockSpec(memory_space=pltpu.VMEM)],
        out_specs=pl.BlockSpec(memory_space=pl.ANY),
        scratch_shapes=[
            pltpu.VMEM((6, rows // 8, cols), BF16),
            pltpu.VMEM((2, rows // 8, cols), BF16),
            pltpu.VMEM((rows // 4, cols), BF16),
            pltpu.VMEM((15, rows // 64, cols), BF16),
            pltpu.VMEM((rows // 64, cols), BF16),
            *[dma((n,)) for n in pairs],
            dma,
        ],
        compiler_params=pltpu.CompilerParams(
            collective_id=0, has_side_effects=True, vmem_limit_bytes=32 << 20
        ),
        name="sum_and_spread",
    )(part)


def apply_kernel(genes, gram, start, out, first, left):
    pieces, rows, width = gram.shape
    block = rows // 2
    trace = F32(0)
    for a in range(pieces):
        h, o = a // 2, (a % 2) * block
        tile = gram[a, h * block : (h + 1) * block, o : o + block].astype(F32)
        spot = lax.broadcasted_iota(jnp.int32, tile.shape, 0)
        spot = spot == lax.broadcasted_iota(jnp.int32, tile.shape, 1)
        trace += jnp.sum(jnp.where(spot, tile, F32(0)))
    scale = jnp.full((1, LANES), trace / genes + 1e-06, F32)
    inverse = 1.0 / scale
    rsqrt = 1.0 / jnp.sqrt(scale)

    def image(a):
        value = jnp.dot(gram[a, :block], left[:width], preferred_element_type=F32)
        value += jnp.dot(gram[a, block:], left[width:], preferred_element_type=F32)
        return value * inverse

    left[...] = start[...]

    @pl.loop(0, pieces)
    def _(a):
        at = pl.ds(pl.multiple_of(a * block, block), block)
        first[at, :] = (1.5 * start[at, :].astype(F32) - 0.5 * image(a)).astype(BF16)

    left[...] = first[...]

    @pl.loop(0, pieces)
    def _(a):
        at = pl.ds(pl.multiple_of(a * block, block), block)
        first[at, :] = image(a).astype(BF16)

    left[...] = first[...]

    @pl.loop(0, pieces)
    def _(a):
        at = pl.ds(pl.multiple_of(a * block, block), block)
        inner = 1.5 * left[at, :].astype(F32) - 0.5 * image(a)
        first[at, :] = (1.5 * start[at, :].astype(F32) - 0.5 * inner).astype(BF16)

    left[...] = first[...]

    @pl.loop(0, pieces)
    def _(a):
        at = pl.ds(pl.multiple_of(a * block, block), block)
        value = 1.5 * left[at, :].astype(F32) - 0.5 * image(a)
        out[at, :] = (value * rsqrt).astype(BF16)


def applied(gram, start, genes):
    vmem = pl.BlockSpec(memory_space=pltpu.VMEM)
    return pl.pallas_call(
        functools.partial(apply_kernel, genes),
        out_shape=jax.ShapeDtypeStruct(start.shape, BF16),
        in_specs=[vmem, vmem],
        out_specs=vmem,
        scratch_shapes=[pltpu.VMEM(start.shape, BF16)] * 2,
        compiler_params=pltpu.CompilerParams(vmem_limit_bytes=48 << 20),
        name="whiten_rows",
    )(gram, start)


def shards(dosage, pheno, perm, snp_weight):
    snps, own = dosage.shape
    genes = pheno.shape[1]
    groups = lax.axis_size(SAMP)
    samples = own * groups
    total_snps = snps * lax.axis_size(SNP)
    nulls = perm.shape[0]
    copies = nulls + 1
    rows = copies * snps
    cols = genes // groups
    me = lax.axis_index(SAMP)
    coded = jnp.concatenate(
        [dosage, perm // LOW, perm % LOW], axis=0
    ).astype(BF16)
    coded = copies_from(coded, SAMP)
    coded = jnp.moveaxis(coded, 0, 1).reshape(coded.shape[1], samples)
    pheno_parts = jnp.moveaxis(pheno.reshape(own, groups, cols), 1, 0)
    pheno_cols = sent_parts(pheno_parts, SAMP).reshape(samples, cols)
    dose = coded[:snps]
    high = coded[snps : snps + nulls]
    low = coded[snps + nulls :]
    steps = samples // LOW
    step_ids = jnp.arange(steps).astype(BF16)[:, None, None]
    low_ids = jnp.arange(LOW).astype(BF16)[:, None]
    placed = [dose]
    for k in range(nulls):
        masked = jnp.where(high[k][None, None, :] == step_ids, dose[None], jnp.zeros((), BF16))
        onehot = (low[k][None, :] == low_ids).astype(BF16)
        part = lax.dot_general(
            masked.reshape(steps * snps, samples), onehot, NT, preferred_element_type=F32
        ).astype(BF16)
        part = part.reshape(steps, snps, LOW)
        placed.append(jnp.concatenate([part[h] for h in range(steps)], axis=1))
    placed = jnp.concatenate(placed, axis=0)
    raw = jnp.dot(placed, pheno_cols, preferred_element_type=F32)
    dose32 = dose.astype(F32)
    dose_mean = jnp.sum(dose32, axis=1) / samples
    dose_square = jnp.sum(dose32 * dose32, axis=1) / samples
    pheno_sum = jnp.sum(pheno_cols.astype(F32), axis=0)
    spread_rows = jnp.sqrt(samples * (dose_square + 1e-05))
    mean_rows = jnp.tile(dose_mean, copies)[:, None]
    spread_rows = jnp.tile(spread_rows, copies)[:, None]
    scores = ((raw - mean_rows * pheno_sum[None, :]) / spread_rows).astype(BF16)
    every = copies_from(scores, SAMP)
    every = jnp.moveaxis(every, 0, 1).reshape(rows, genes)
    weight_rows = jnp.tile(snp_weight, nulls)[:, None]
    weighted = (every[snps:].astype(F32) * weight_rows).astype(BF16)
    width = genes // 2
    part = jnp.concatenate(
        [
            lax.dot_general(
                scores[snps:], weighted[:, h * width : (h + 1) * width], TN,
                preferred_element_type=F32,
            ).astype(BF16)
            for h in range(2)
        ],
        axis=0,
    )
    gram = spread(part, nulls * total_snps)
    share = rows // groups
    mine = lax.dynamic_slice_in_dim(every, me * share, share, 0)
    start = jnp.pad(mine.T, ((0, 0), (0, LANES - share)))
    white = applied(gram, start, genes)[:, :share].T
    white = white.reshape(share, groups, cols)
    white = sent_parts(jnp.moveaxis(white, 1, 0), SAMP)
    return white.reshape(copies, snps, cols)


def solution(mesh):
    finer = Mesh(mesh.devices.reshape(2, 2, 4, 8, 2), (*SAMP, *SNP))
    in_specs = (P(SNP, SAMP), P(SAMP, None), P(None, SAMP), P(SNP))
    return jax.shard_map(
        shards, mesh=finer, in_specs=in_specs, out_specs=P(None, SNP, SAMP), check_vma=False
    )
```

time: 371 us -> 228 us (0.61)
  Pallas kernels: 0 us -> 103 us
  blocking collectives: 109 us -> 9.81 us
  waiting for transfers between devices: 113 us -> 22.5 us
  matrix products: 43.9 us -> 11.2 us
  starting transfers between devices: 28.6 us -> 15.7 us
  other arithmetic: 9.98 us -> 5.26 us
    pallas_call x0 -> x2, Pallas kernels: none -> 103 us  [the longest x1 87.4 us: spread(): pl.pallas_call(functools.partial(spread_kernel, total), out_shape=jax.Sha...]
    all_to_all x7 -> x1, blocking collectives: 109 us -> 9.81 us  [sent_parts(): return lax.all_to_all(array, axis, split_axis=0, concat_axis=0, tiled=True)]
    all_to_all x4 -> x3, waiting for transfers between devices: 113 us -> 22.5 us  [sent_parts(): return lax.all_to_all(array, axis, split_axis=0, concat_axis=0, tiled=True)]
    dot_general x17 -> x2, matrix products: 34.2 us -> 1.51 us  [shards(): lax.dot_general(scores[snps:], weighted[:, h * width:(h + 1) * width], TN...]
    all_to_all x4 -> x3, starting transfers between devices: 28.6 us -> 15.7 us  [sent_parts(): return lax.all_to_all(array, axis, split_axis=0, concat_axis=0, tiled=True)]
    reduce_sum x4 -> x0, other arithmetic: 4.57 us -> none  [the longest x3 2.31 us: summed_share(): return jnp.sum(arrived.astype(F32), axis=0)]
    broadcast_in_dim x6 -> x2, local copies, waits for them, and re-layouts: 6.17 us -> 2.06 us  [copies_from(): jnp.broadcast_to(array[None], (devices, *array.shape))]
    unnamed x88 -> x90, local copies, waits for them, and re-layouts: 44.5 us -> 47.9 us
  transfers between devices with their start and end apart: 4 -> 3, of which waited for: 3 -> 2; matrix products, arithmetic and copies ran while one was open for 15% -> 24% of each run, Pallas kernels for 0% -> 0%
where the time goes in v2:
time: 228 us; the launch traced here: 227 us
  Pallas kernels  103 us (45%)
  local copies, waits for them, and re-layouts  59.6 us (26%)
  waiting for transfers between devices  22.5 us (10%)
  starting transfers between devices  15.7 us (7%)
  matrix products  11.2 us (5%)
  blocking collectives  9.81 us (4%)
  other arithmetic  5.26 us (2%)
    pallas_call x1, Pallas kernels, spread(): pl.pallas_call(functools.partial(spread_kernel, total), out_shape=jax.Sha...  87.4 us
    unnamed x90, local copies, waits for them, and re-layouts  47.9 us
    all_to_all x3, waiting for transfers between devices, sent_parts(): return lax.all_to_all(array, axis, split_axis=0, concat_axis=0, tiled=True)  22.5 us
    all_to_all x3, starting transfers between devices, sent_parts(): return lax.all_to_all(array, axis, split_axis=0, concat_axis=0, tiled=True)  15.7 us
    pallas_call x1, Pallas kernels, applied(): pl.pallas_call(functools.partial(apply_kernel, genes), out_shape=jax.Shap...  15.2 us
    all_to_all x1, blocking collectives, sent_parts(): return lax.all_to_all(array, axis, split_axis=0, concat_axis=0, tiled=True)  9.81 us
    dot_general x8, matrix products, shards(): lax.dot_general(masked.reshape(steps * snps, samples), onehot, NT, prefer...  7.14 us
    all_to_all x2, local copies, waits for them, and re-layouts, sent_parts(): return lax.all_to_all(array, axis, split_axis=0, concat_axis=0, tiled=True)  5.1 us
  transfers between devices with their start and end apart: 3, of which 2 were waited for; matrix products, arithmetic and copies ran while one was open for 24% of the time, Pallas kernels for 0%

profile of v2, /device:TPU:1, one launch (start us, length us, event | category | flops | bytes accessed | tf_op | source)
XLA Modules:
  0.0 227.1 jit_solution(10547386588005892921)
XLA Ops:
  0.0 0.7 fusion.64
  0.7 0.9 convert.10
  1.7 0.7 broadcast_in_dim.106
  2.4 6.6 %all-to-all-start = ((bf16[4,64,512]{2,1,0:T(8,128)(2,1)}), bf16[4,64,512]{2,1,0:T(8,128)(2,1)S(1)}, u32[]{:S(2)}, u32[]{:S(2)}) async-start(bf16[4,64,512]{2,1,0:T(8,128)(2,1)} %broadcast_in_dim.106), calls=%async_computation | async-start | bytes 524288 | tf_op jit(solution)/shard_map/all_to_all | solution.py:23
  9.0 3.9 %copy.19 = bf16[512,2048]{0,1:T(8,128)(2,1)} copy(bf16[512,2048]{1,0:T(8,128)(2,1)} %param.5) | data formatting | bytes 4194304 | tf_op args[1]
  12.9 1.2 all-to-all-done
  14.2 4.4 %all-to-all-start.1 = ((bf16[4,512,512]{1,2,0:T(8,128)(2,1)}), bf16[4,512,512]{1,2,0:T(8,128)(2,1)S(1)}, u32[]{:S(2)}, u32[]{:S(2)}) async-start(bf16[4,512,512]{1,2,0:T(8,128)(2,1)} %bitcast.72), calls=%async_computation.1 | async-start | bytes 4194304 | tf_op jit(solution)/shard_map/all_to_all | solution.py:23
  19.2 0.7 constant_dynamic-update-slice_fusion
  20.1 2.3 %broadcast_select_fusion = (bf16[8,48,2048]{2,1,0:T(8,128)(2,1)}, bf16[8,48,2048]{2,1,0:T(8,128)(2,1)S(1)}, bf16[8,48,2048]{2,1,0:T(8,128)(2,1)S(1)}, bf16[8,48,...) fusion(pred[8,2048]{1,0:T(8,128)(4,1)S(1)} %get-tuple-element.3, ...), kind=kLoop, calls=%fused_computation.20 | loop fusion | flops 6291456 | bytes 12910592 | tf_op jit(solution)/shard_map/jit(_where)/select_n | solution.py:298
  22.4 0.7 fusion.19
  28.0 0.7 fusion.22
  30.5 0.6 slice_dynamic-update-slice_fusion.52
  33.6 0.7 fusion.25
  36.1 0.6 slice_dynamic-update-slice_fusion.44
  39.2 0.7 fusion.28
  41.1 0.6 slice_dynamic-update-slice_fusion.37
  43.0 0.6 slice_dynamic-update-slice_fusion.34
  44.8 0.7 fusion.31
  45.5 0.6 slice_dynamic-update-slice_fusion.31
  49.2 0.6 slice_dynamic-update-slice_fusion.25
  49.8 0.6 slice_dynamic-update-slice_fusion.24
  50.5 0.7 fusion.34
  51.8 0.6 slice_dynamic-update-slice_fusion.22
  56.1 0.7 fusion.37
  56.8 0.6 slice_dynamic-update-slice_fusion.15
  58.6 0.6 slice_dynamic-update-slice_fusion.12
  59.3 0.6 slice_dynamic-update-slice_fusion.11
  59.9 0.6 slice_dynamic-update-slice_fusion.10
  61.9 2.1 fusion.40
  66.5 0.6 slice_dynamic-update-slice_fusion.3
  67.1 0.6 slice_dynamic-update-slice_fusion.2
  67.7 0.6 slice_dynamic-update-slice_fusion.1
  69.0 2.4 %copy.20 = bf16[4,512,512]{2,1,0:T(8,128)(2,1)} copy(bf16[4,512,512]{1,2,0:T(8,128)(2,1)S(1)} %all-to-all-done.1) | data formatting | bytes 4194304 | tf_op jit(solution)/shard_map/all_to_all | solution.py:23
  71.7 1.2 copy-done.2
  73.0 2.6 %fusion.18 = bf16[432,512]{1,0:T(8,128)(2,1)S(1)} fusion(bf16[432,2048]{1,0:T(8,128)(2,1)} %slice_dynamic-update-slice_fusion, bf16[2048,512]{1,0:T(8,128)(2,1)S(1)} %bitcast.78, f32[432]{0:T(512)S(1)} %div.34, f32[512]{0:T(512)S(1)} %convert_reduce_fusion, f32[432]{0:T(512)S(1)} %mul.42), kind=kOutput, calls=%fused_computation.32 | convolution fusion | flops 906854400 | bytes 4314496 | tf_op jit(solution)/shard_map/dot_general | solution.py:306
  75.5 1.3 broadcast_in_dim.117
  76.9 4.7 %all-to-all-start.2 = ((bf16[4,432,512]{2,1,0:T(8,128)(2,1)}), bf16[4,432,512]{2,1,0:T(8,128)(2,1)}, u32[]{:S(2)}, u32[]{:S(2)}) async-start(bf16[4,432,512]{2,1,0:T(8,128)(2,1)} %broadcast_in_dim.117), calls=%async_computation.2 | async-start | bytes 3538944 | tf_op jit(solution)/shard_map/all_to_all | solution.py:23
  81.7 21.3 %all-to-all-done.2 = bf16[4,432,512]{2,1,0:T(8,128)(2,1)} async-done(((bf16[4,432,512]{2,1,0:T(8,128)(2,1)}), bf16[4,432,512]{2,1,0:T(8,128)(2,1)}, u32[]{:S(2)}, u32[]{:S(2)}) %all-to-all-start.2) | async-done | bytes 1769504 | tf_op jit(solution)/shard_map/all_to_all | solution.py:23
  103.0 2.7 %copy.21 = bf16[4,432,512]{1,2,0:T(8,128)(2,1)S(1)} copy(bf16[4,432,512]{2,1,0:T(8,128)(2,1)} %all-to-all-done.2) | data formatting | bytes 3538944 | tf_op jit(solution)/shard_map/all_to_all | solution.py:23
  105.7 0.7 slice.532
  107.1 0.8 convolution_convert_fusion.1
  107.9 0.8 convolution_convert_fusion
  108.8 87.4 %sum_and_spread.1.gram = bf16[4,1024,1024]{2,1,0:T(8,128)(2,1)S(1)} custom-call(bf16[1024,1024]{1,0:T(8,128)(2,1)S(1)} %pad_maximum_fusion.part), custom_call_target="tpu_custom_call" | custom-call | tf_op jit(solution)/shard_map/sum_and_spread/pallas_call | solution.py:188
  196.2 3.2 %copy-done = bf16[4,1024,1024]{2,1,0:T(8,128)(2,1)} copy-done((bf16[4,1024,1024]{2,1,0:T(8,128)(2,1)}, bf16[4,1024,1024]{2,1,0:T(8,128)(2,1)S(1)}, u32[]{:S(2)}) %copy-start) | copy-done | bytes 8388632
  199.4 1.4 dynamic-slice_bitcast_fusion
  200.9 15.2 %whiten_rows.1 = bf16[2048,128]{1,0:T(8,128)(2,1)S(1)} custom-call(bf16[4,1024,1024]{2,1,0:T(8,128)(2,1)} %copy-done, bf16[2048,128]{1,0:T(8,128)(2,1)S(1)} %pad.4.start), custom_call_target="tpu_custom_call" | custom-call | tf_op jit(solution)/shard_map/whiten_rows/pallas_call | solution.py:261
  216.4 9.8 %all_to_all.20 = bf16[4,108,512]{2,1,0:T(8,128)(2,1)S(1)} all-to-all(bf16[4,108,512]{2,1,0:T(8,128)(2,1)S(1)} %bitcast.79), channel_id=1, replica_groups=mesh['y_lo'=2,'core'=2,'x'=4,'z'=8,'y_hi'=2] {'y_lo','core'}, dimensions={0} | all-to-all | bytes 884736 | tf_op jit(solution)/shard_map/all_to_all | solution.py:23
  226.2 0.8 reshape.523
  (92 shorter events, 32.3 us)
Async XLA Ops:
  2.4 11.8 %all-to-all-start = ((bf16[4,64,512]{2,1,0:T(8,128)(2,1)}), bf16[4,64,512]{2,1,0:T(8,128)(2,1)S(1)}, u32[]{:S(2)}, u32[]{:S(2)}) async-start(bf16[4,64,512]{2,1,0:T(8,128)(2,1)} %broadcast_in_dim.106), calls=%async_computation | async-start | bytes 524288 | tf_op jit(solution)/shard_map/all_to_all | solution.py:23
  14.2 54.8 %all-to-all-start.1 = ((bf16[4,512,512]{1,2,0:T(8,128)(2,1)}), bf16[4,512,512]{1,2,0:T(8,128)(2,1)S(1)}, u32[]{:S(2)}, u32[]{:S(2)}) async-start(bf16[4,512,512]{1,2,0:T(8,128)(2,1)} %bitcast.72), calls=%async_computation.1 | async-start | bytes 4194304 | tf_op jit(solution)/shard_map/all_to_all | solution.py:23
  71.4 1.6 copy-start.2
  76.9 4.7 %copy-start.3 = (f32[48]{0:T(128)S(1)}, f32[48]{0:T(128)}, u32[]{:S(2)}) copy-start(f32[48]{0:T(128)} %param.7) | copy-start | bytes 580
  76.9 26.1 %all-to-all-start.2 = ((bf16[4,432,512]{2,1,0:T(8,128)(2,1)}), bf16[4,432,512]{2,1,0:T(8,128)(2,1)}, u32[]{:S(2)}, u32[]{:S(2)}) async-start(bf16[4,432,512]{2,1,0:T(8,128)(2,1)} %broadcast_in_dim.117), calls=%async_computation.2 | async-start | bytes 3538944 | tf_op jit(solution)/shard_map/all_to_all | solution.py:23
  105.7 1.4 copy-start.1
  196.2 3.2 %copy-start = (bf16[4,1024,1024]{2,1,0:T(8,128)(2,1)}, bf16[4,1024,1024]{2,1,0:T(8,128)(2,1)S(1)}, u32[]{:S(2)}) copy-start(bf16[4,1024,1024]{2,1,0:T(8,128)(2,1)S(1)} %sum_and_spread.1.gram) | copy-start | bytes 25165828

commit v3 on v2

--- a/solution.py
+++ b/solution.py
@@ -13,7 +13,6 @@
 F32 = jnp.float32
 BF16 = jnp.bfloat16
 NT = (((1,), (1,)), ((), ()))
-TN = (((0,), (0,)), ((), ()))
 LOW = 256
 MESH = pl.DeviceIdType.MESH
 LANES = 128
@@ -21,11 +20,6 @@
 
 def sent_parts(array, axis):
     return lax.all_to_all(array, axis, split_axis=0, concat_axis=0, tiled=True)
-
-
-def copies_from(array, axis):
-    devices = lax.axis_size(axis)
-    return sent_parts(jnp.broadcast_to(array[None], (devices, *array.shape)), axis)
 
 
 def spread_kernel(
@@ -206,13 +200,193 @@
     )(part)
 
 
+def front_kernel(
+    dosage, pheno, perm, weight_rows, part, every,
+    coded, codes, placed, cols_in, turned,
+    a_send, a_recv, p_send, p_recv, s_send, s_recv, n_send, n_recv, f_send, f_recv, own_sem,
+):
+    snps, own = dosage.shape
+    nulls = perm.shape[0]
+    samples, cols = cols_in.shape
+    copies = nulls + 1
+    rows = copies * snps
+    lead = placed.shape[0] - rows
+    y_lo, core, y_hi = lax.axis_index("y_lo"), lax.axis_index("core"), lax.axis_index("y_hi")
+    me = y_lo * 2 + core
+    sib_id = y_lo * 2 + 1 - core
+    near_id = (1 - y_lo) * 2 + core
+    cross_id = (1 - y_lo) * 2 + 1 - core
+    sibling = {"core": 1 - core}
+    near = {"y_lo": 1 - y_lo}
+    cross = {"y_lo": 1 - y_lo, "core": 1 - core}
+    far = {"y_lo": 1 - y_lo, "y_hi": 1 - y_hi}
+    far_cross = {"y_lo": 1 - y_lo, "y_hi": 1 - y_hi, "core": 1 - core}
+
+    def span(index, size):
+        return pl.ds(pl.multiple_of(index * size, size), size)
+
+    barrier = pltpu.get_barrier_semaphore()
+    greeted = (sibling, near, cross, far, far_cross)
+    for there in greeted:
+        pl.semaphore_signal(barrier, inc=1, device_id=there, device_id_type=MESH)
+    mine = span(me, own)
+    coded[:snps, mine] = dosage[...].astype(F32).astype(BF16)
+    source = perm[...]
+    both = jnp.concatenate([lax.shift_right_logical(source, 8), source & 255], axis=0)
+    coded[snps:, mine] = both.astype(F32).astype(BF16)
+    pl.semaphore_wait(barrier, len(greeted))
+
+    started = []
+
+    def send(src, dst, send_sem, recv_sem, there):
+        copy = pltpu.make_async_remote_copy(
+            src_ref=src, dst_ref=dst, send_sem=send_sem, recv_sem=recv_sem,
+            device_id=there, device_id_type=MESH,
+        )
+        copy.start()
+        started.append(copy)
+        return copy
+
+    coming = [
+        send(coded.at[:, mine], coded.at[:, mine], a_send.at[i], a_recv.at[i], there)
+        for i, there in enumerate((near, cross, sibling))
+    ]
+    half = own // 2
+    pheno_coming = []
+    for i, (there, target, h) in enumerate(
+        ((near, near_id, 0), (cross, cross_id, 0), (far, near_id, 1), (far_cross, cross_id, 1))
+    ):
+        pheno_coming.append(
+            send(
+                pheno.at[pl.ds(h * half, half), span(target, cols)],
+                cols_in.at[pl.ds(pl.multiple_of(me * own + h * half, half), half)],
+                p_send.at[i], p_recv.at[i], there,
+            )
+        )
+    pheno_coming.append(
+        send(
+            pheno.at[:, span(sib_id, cols)], cols_in.at[span(me, own)],
+            p_send.at[4], p_recv.at[4], sibling,
+        )
+    )
+    stay = pltpu.make_async_copy(pheno.at[:, span(me, cols)], cols_in.at[span(me, own)], own_sem)
+    stay.start()
+    placed[:lead, :] = jnp.ones((lead, samples), BF16)
+    for copy in coming:
+        copy.wait_recv()
+
+    codes[...] = coded[snps:, :].astype(F32)
+    dose = coded[:snps, :]
+    placed[lead : lead + snps, :] = dose
+    dose32 = dose.astype(F32)
+    dose_mean = jnp.sum(dose32, axis=1, keepdims=True) / samples
+    dose_square = jnp.sum(dose32 * dose32, axis=1, keepdims=True) / samples
+    spread_rows = jnp.sqrt(samples * (dose_square + 1e-05))
+    steps = samples // LOW
+
+    @pl.loop(0, nulls)
+    def _(k):
+        high = codes[pl.ds(k, 1), :]
+        low = codes[pl.ds(nulls + k, 1), :]
+        values = coded[:snps, :]
+        masked = jnp.concatenate(
+            [values * (high == F32(h)).astype(F32).astype(BF16) for h in range(steps)], axis=0
+        )
+        ids = lax.broadcasted_iota(jnp.int32, (LOW, samples), 0).astype(F32)
+        onehot = (ids == low).astype(F32).astype(BF16)
+        got = lax.dot_general(masked, onehot, NT, preferred_element_type=F32).astype(BF16)
+        at = pl.ds(pl.multiple_of(lead + (k + 1) * snps, 16), snps)
+        for h in range(steps):
+            placed[at, h * LOW : (h + 1) * LOW] = got[h * snps : (h + 1) * snps]
+
+    stay.wait()
+    for copy in pheno_coming:
+        copy.wait_recv()
+
+    chunks = 3
+    per = copies // chunks
+    total = None
+    to_sib, to_near = [], []
+    for c in range(chunks):
+        first = 0 if c == 0 else lead + c * per * snps
+        last = lead + (c + 1) * per * snps
+        raw = jnp.dot(placed[first:last, :], cols_in[...], preferred_element_type=F32)
+        if c == 0:
+            total = raw[:1]
+            raw = raw[lead:]
+        for j in range(per):
+            value = (raw[j * snps : (j + 1) * snps] - dose_mean * total) / spread_rows
+            at = (c * per + j) * snps
+            every[me, at : at + snps] = value.astype(BF16)
+        sent = pl.ds(c * per * snps, per * snps)
+        block = every.at[me, sent]
+        to_near.append(send(block, block, n_send.at[c], n_recv.at[c], near))
+        to_sib.append(send(block, block, s_send.at[c], s_recv.at[c], sibling))
+
+    turned[...] = every[me, snps:].astype(F32).T.astype(BF16)
+
+    def share(which):
+        weighted = (every[which, snps:].astype(F32) * weight_rows[...]).astype(BF16)
+        part[span(which, cols), :] = jnp.dot(
+            turned[...], weighted, preferred_element_type=F32
+        ).astype(BF16)
+
+    share(me)
+    for copy in to_sib:
+        copy.wait_recv()
+    share(sib_id)
+    passed = []
+    for c in range(chunks):
+        to_near[c].wait_recv()
+        block = every.at[near_id, pl.ds(c * per * snps, per * snps)]
+        passed.append(send(block, block, f_send.at[c], f_recv.at[c], sibling))
+    share(near_id)
+    for copy in passed:
+        copy.wait_recv()
+    share(cross_id)
+    for copy in started:
+        copy.wait_send()
+
+
+def front(dosage, pheno, perm, weight_rows):
+    snps, own = dosage.shape
+    genes = pheno.shape[1]
+    nulls = perm.shape[0]
+    rows = (nulls + 1) * snps
+    samples, cols = own * 4, genes // 4
+    lead = 16
+    dma = pltpu.SemaphoreType.DMA
+    vmem = pl.BlockSpec(memory_space=pltpu.VMEM)
+    pairs = [3, 3, 5, 5, 3, 3, 3, 3, 3, 3]
+    return pl.pallas_call(
+        front_kernel,
+        out_shape=(
+            jax.ShapeDtypeStruct((genes, cols), BF16),
+            jax.ShapeDtypeStruct((4, rows, cols), BF16),
+        ),
+        in_specs=[vmem, pl.BlockSpec(memory_space=pl.ANY), vmem, vmem],
+        out_specs=(vmem, vmem),
+        scratch_shapes=[
+            pltpu.VMEM((snps + 2 * nulls, samples), BF16),
+            pltpu.VMEM((2 * nulls, samples), F32),
+            pltpu.VMEM((lead + rows, samples), BF16),
+            pltpu.VMEM((samples, cols), BF16),
+            pltpu.VMEM((cols, rows - snps), BF16),
+            *[dma((n,)) for n in pairs],
+            dma,
+        ],
+        compiler_params=pltpu.CompilerParams(
+            collective_id=1, has_side_effects=True, vmem_limit_bytes=40 << 20
+        ),
+        name="scores_and_gram_share",
+    )(dosage, pheno, perm, weight_rows)
+
+
 def apply_kernel(genes, gram, start, out, first, left):
-    pieces, rows, width = gram.shape
-    block = rows // 2
+    pieces, rows, block = gram.shape
     trace = F32(0)
     for a in range(pieces):
-        h, o = a // 2, (a % 2) * block
-        tile = gram[a, h * block : (h + 1) * block, o : o + block].astype(F32)
+        tile = gram[a, a * block : (a + 1) * block].astype(F32)
         spot = lax.broadcasted_iota(jnp.int32, tile.shape, 0)
         spot = spot == lax.broadcasted_iota(jnp.int32, tile.shape, 1)
         trace += jnp.sum(jnp.where(spot, tile, F32(0)))
@@ -221,8 +395,11 @@
     rsqrt = 1.0 / jnp.sqrt(scale)
 
     def image(a):
-        value = jnp.dot(gram[a, :block], left[:width], preferred_element_type=F32)
-        value += jnp.dot(gram[a, block:], left[width:], preferred_element_type=F32)
+        value = None
+        for b in range(pieces):
+            at = slice(b * block, (b + 1) * block)
+            one = jnp.dot(gram[a, at], left[at], preferred_element_type=F32)
+            value = one if value is None else value + one
         return value * inverse
 
     left[...] = start[...]
@@ -270,67 +447,21 @@
 
 
 def shards(dosage, pheno, perm, snp_weight):
-    snps, own = dosage.shape
+    snps = dosage.shape[0]
     genes = pheno.shape[1]
     groups = lax.axis_size(SAMP)
-    samples = own * groups
-    total_snps = snps * lax.axis_size(SNP)
     nulls = perm.shape[0]
     copies = nulls + 1
     rows = copies * snps
     cols = genes // groups
     me = lax.axis_index(SAMP)
-    coded = jnp.concatenate(
-        [dosage, perm // LOW, perm % LOW], axis=0
-    ).astype(BF16)
-    coded = copies_from(coded, SAMP)
-    coded = jnp.moveaxis(coded, 0, 1).reshape(coded.shape[1], samples)
-    pheno_parts = jnp.moveaxis(pheno.reshape(own, groups, cols), 1, 0)
-    pheno_cols = sent_parts(pheno_parts, SAMP).reshape(samples, cols)
-    dose = coded[:snps]
-    high = coded[snps : snps + nulls]
-    low = coded[snps + nulls :]
-    steps = samples // LOW
-    step_ids = jnp.arange(steps).astype(BF16)[:, None, None]
-    low_ids = jnp.arange(LOW).astype(BF16)[:, None]
-    placed = [dose]
-    for k in range(nulls):
-        masked = jnp.where(high[k][None, None, :] == step_ids, dose[None], jnp.zeros((), BF16))
-        onehot = (low[k][None, :] == low_ids).astype(BF16)
-        part = lax.dot_general(
-            masked.reshape(steps * snps, samples), onehot, NT, preferred_element_type=F32
-        ).astype(BF16)
-        part = part.reshape(steps, snps, LOW)
-        placed.append(jnp.concatenate([part[h] for h in range(steps)], axis=1))
-    placed = jnp.concatenate(placed, axis=0)
-    raw = jnp.dot(placed, pheno_cols, preferred_element_type=F32)
-    dose32 = dose.astype(F32)
-    dose_mean = jnp.sum(dose32, axis=1) / samples
-    dose_square = jnp.sum(dose32 * dose32, axis=1) / samples
-    pheno_sum = jnp.sum(pheno_cols.astype(F32), axis=0)
-    spread_rows = jnp.sqrt(samples * (dose_square + 1e-05))
-    mean_rows = jnp.tile(dose_mean, copies)[:, None]
-    spread_rows = jnp.tile(spread_rows, copies)[:, None]
-    scores = ((raw - mean_rows * pheno_sum[None, :]) / spread_rows).astype(BF16)
-    every = copies_from(scores, SAMP)
-    every = jnp.moveaxis(every, 0, 1).reshape(rows, genes)
     weight_rows = jnp.tile(snp_weight, nulls)[:, None]
-    weighted = (every[snps:].astype(F32) * weight_rows).astype(BF16)
-    width = genes // 2
-    part = jnp.concatenate(
-        [
-            lax.dot_general(
-                scores[snps:], weighted[:, h * width : (h + 1) * width], TN,
-                preferred_element_type=F32,
-            ).astype(BF16)
-            for h in range(2)
-        ],
-        axis=0,
-    )
-    gram = spread(part, nulls * total_snps)
+    part, every = front(dosage, pheno, perm, weight_rows)
+    gram = spread(part, nulls * snps * lax.axis_size(SNP))
     share = rows // groups
-    mine = lax.dynamic_slice_in_dim(every, me * share, share, 0)
-    start = jnp.pad(mine.T, ((0, 0), (0, LANES - share)))
+    mine = lax.dynamic_slice_in_dim(every, me * share, share, 1)
+    start = jnp.swapaxes(mine, 1, 2).reshape(genes, share)
+    start = jnp.pad(start, ((0, 0), (0, LANES - share)))
     white = applied(gram, start, genes)[:, :share].T
     white = white.reshape(share, groups, cols)
     white = sent_parts(jnp.moveaxis(white, 1, 0), SAMP)

time: 228 us -> 156 us (0.68)
  local copies, waits for them, and re-layouts: 59.6 us -> 8.8 us
  Pallas kernels: 103 us -> 137 us
  waiting for transfers between devices: 22.5 us -> 0 us
  starting transfers between devices: 15.7 us -> 0 us
  matrix products: 11.2 us -> 0 us
  other arithmetic: 5.26 us -> 0 us
    unnamed x90 -> x8, local copies, waits for them, and re-layouts: 47.9 us -> 6.4 us
    pallas_call x0 -> x1, Pallas kernels: none -> 34 us  [front(): pl.pallas_call(front_kernel, out_shape=(jax.ShapeDtypeStruct((genes, cols...]
    all_to_all x3 -> x0, waiting for transfers between devices: 22.5 us -> none  [sent_parts(): return lax.all_to_all(array, axis, split_axis=0, concat_axis=0, tiled=True)]
    all_to_all x3 -> x0, starting transfers between devices: 15.7 us -> none  [sent_parts(): return lax.all_to_all(array, axis, split_axis=0, concat_axis=0, tiled=True)]
    dot_general x11 -> x0, matrix products: 11.2 us -> none  [the longest x8 7.14 us: shards(): lax.dot_general(masked.reshape(steps * snps, samples), onehot, NT, prefer...]
    all_to_all x2 -> x0, local copies, waits for them, and re-layouts: 5.1 us -> none  [sent_parts(): return lax.all_to_all(array, axis, split_axis=0, concat_axis=0, tiled=True)]
    select_n x1 -> x0, other arithmetic: 2.28 us -> none  [shards(): jnp.where(high[k][None, None, :] == step_ids, dose[None], jnp.zeros((), B...]
  transfers between devices with their start and end apart: 3 -> 0, of which waited for: 2 -> 0; matrix products, arithmetic and copies ran while one was open for 24% -> 0% of each run, Pallas kernels for 0% -> 0%
where the time goes in v3:
time: 156 us; the launch traced here: 155 us
  Pallas kernels  137 us (88%)
  blocking collectives  9.82 us (6%)
  local copies, waits for them, and re-layouts  8.8 us (6%)
    pallas_call x1, Pallas kernels, spread(): pl.pallas_call(functools.partial(spread_kernel, total), out_shape=jax.Sha...  87.7 us
    pallas_call x1, Pallas kernels, front(): pl.pallas_call(front_kernel, out_shape=(jax.ShapeDtypeStruct((genes, cols...  34 us
    pallas_call x1, Pallas kernels, applied(): pl.pallas_call(functools.partial(apply_kernel, genes), out_shape=jax.Shap...  15.2 us
    all_to_all x1, blocking collectives, sent_parts(): return lax.all_to_all(array, axis, split_axis=0, concat_axis=0, tiled=True)  9.82 us
    unnamed x8, local copies, waits for them, and re-layouts  6.4 us

profile of v3, /device:TPU:1, one launch (start us, length us, event | category | flops | bytes accessed | tf_op | source)
XLA Modules:
  0.0 155.5 jit_solution(13747069540608259432)
XLA Ops:
  0.0 0.7 tile.2
  0.7 0.1 broadcast_in_dim_tile.4.weight_rows
  0.8 0.0 copy-start.1
  0.8 1.6 %copy-done.1 = bf16[512,2048]{1,0:T(8,128)(2,1)S(1)} copy-done((bf16[512,2048]{1,0:T(8,128)(2,1)S(1)}, bf16[512,2048]{1,0:T(8,128)(2,1)}, u32[]{:S(2)}) %copy-start.1) | copy-done | bytes 2097176
  2.4 0.0 copy-start.2
  2.4 0.9 copy-done.2
  3.3 0.0 copy-start.3
  3.3 0.7 copy-done.3
  4.0 34.0 %scores_and_gram_share.1 = (bf16[2048,512]{1,0:T(8,128)(2,1)S(1)}, bf16[4,432,512]{2,1,0:T(8,128)(2,1)S(1)}) custom-call(s32[48,512]{1,0:T(8,128)S(1)} %copy-done.2, bf16[512,2048]{1,0:T(8,128)(2,1)S(1)} %copy-done.1, s32[8,512]{1,0:T(8,128)S(1)} %copy-done.3, f32[384,1]{1,0:T(8,128)S(1)} %broadcast_in_dim_tile.4.weight_rows), custom_call_target="tpu_custom_call" | custom-call | tf_op jit(solution)/shard_map/scores_and_gram_share/pallas_call | solution.py:361
  38.0 0.1 dynamic-slice_bitcast_fusion
  38.1 0.3 copy.8
  38.4 87.7 %sum_and_spread.1.gram = bf16[4,2048,512]{2,1,0:T(8,128)(2,1)S(1)} custom-call(bf16[2048,512]{1,0:T(8,128)(2,1)S(1)} %get-tuple-element.7.part), custom_call_target="tpu_custom_call" | custom-call | tf_op jit(solution)/shard_map/sum_and_spread/pallas_call | solution.py:182
  126.0 0.0 copy-start
  126.1 3.2 %copy-done = bf16[4,2048,512]{2,1,0:T(8,128)(2,1)} copy-done((bf16[4,2048,512]{2,1,0:T(8,128)(2,1)}, bf16[4,2048,512]{2,1,0:T(8,128)(2,1)S(1)}, u32[]{:S(2)}) %copy-start) | copy-done | bytes 8388632
  129.3 0.1 pad.4.start
  129.4 15.2 %whiten_rows.1 = bf16[2048,128]{1,0:T(8,128)(2,1)S(1)} custom-call(bf16[4,2048,512]{2,1,0:T(8,128)(2,1)} %copy-done, bf16[2048,128]{1,0:T(8,128)(2,1)S(1)} %pad.4.start), custom_call_target="tpu_custom_call" | custom-call | tf_op jit(solution)/shard_map/whiten_rows/pallas_call | solution.py:438
  144.6 0.3 copy.9
  144.8 9.8 %all_to_all.5 = bf16[4,108,512]{2,1,0:T(8,128)(2,1)S(1)} all-to-all(bf16[4,108,512]{2,1,0:T(8,128)(2,1)S(1)} %bitcast.10), channel_id=1, replica_groups=mesh['y_lo'=2,'core'=2,'x'=4,'z'=8,'y_hi'=2] {'y_lo','core'}, dimensions={0} | all-to-all | bytes 884736 | tf_op jit(solution)/shard_map/all_to_all | solution.py:22
  154.6 0.8 reshape.12
Async XLA Ops:
  0.8 1.6 %copy-start.1 = (bf16[512,2048]{1,0:T(8,128)(2,1)S(1)}, bf16[512,2048]{1,0:T(8,128)(2,1)}, u32[]{:S(2)}) copy-start(bf16[512,2048]{1,0:T(8,128)(2,1)} %pheno.1) | copy-start | bytes 6291460
  2.4 0.9 copy-start.2
  3.3 0.7 copy-start.3
  126.0 3.2 %copy-start = (bf16[4,2048,512]{2,1,0:T(8,128)(2,1)}, bf16[4,2048,512]{2,1,0:T(8,128)(2,1)S(1)}, u32[]{:S(2)}) copy-start(bf16[4,2048,512]{2,1,0:T(8,128)(2,1)S(1)} %sum_and_spread.1.gram) | copy-start | bytes 25165828

commit v4 on v1

v4 whole, which is shorter than its diff:
```python
import functools

import jax
import jax.numpy as jnp
from jax import lax
from jax.experimental import pallas as pl
from jax.experimental.pallas import tpu as pltpu
from jax.sharding import Mesh
from jax.sharding import PartitionSpec as P

SAMP = ("y_lo", "core")
SNP = ("x", "z", "y_hi")
F32 = jnp.float32
BF16 = jnp.bfloat16
NT = (((1,), (1,)), ((), ()))
LOW = 256
TILE = 256
WIDE = 640
LANES = 128
LEAD = 16
CHUNKS = 3
MESH = pl.DeviceIdType.MESH


def span(index, size):
    return pl.ds(pl.multiple_of(index * size, size), size)


class Sender:
    def __init__(self):
        self.started = []

    def __call__(self, src, dst, sems, i, there):
        copy = pltpu.make_async_remote_copy(
            src_ref=src, dst_ref=dst, send_sem=sems[0].at[i], recv_sem=sems[1].at[i],
            device_id=there, device_id_type=MESH,
        )
        copy.start()
        self.started.append(copy)
        return copy

    def finish(self):
        for copy in self.started:
            copy.wait_send()


class Place:
    def __init__(self):
        x, z, y_hi = lax.axis_index("x"), lax.axis_index("z"), lax.axis_index("y_hi")
        y_lo, core = lax.axis_index("y_lo"), lax.axis_index("core")
        self.x, self.z, self.y_hi, self.y_lo, self.core = x, z, y_hi, y_lo, core
        self.me = y_lo * 2 + core
        self.sib_id = y_lo * 2 + 1 - core
        self.near_id = (1 - y_lo) * 2 + core
        self.cross_id = (1 - y_lo) * 2 + 1 - core
        self.sibling = {"core": 1 - core}
        self.near = {"y_lo": 1 - y_lo}
        self.cross = {"y_lo": 1 - y_lo, "core": 1 - core}
        self.far = {"y_lo": 1 - y_lo, "y_hi": 1 - y_hi}
        self.far_cross = {"y_lo": 1 - y_lo, "y_hi": 1 - y_hi, "core": 1 - core}
        self.right, self.left = lax.rem(x + 1, 4), lax.rem(x + 3, 4)
        self.across = lax.rem(x + 2, 4)
        self.to_right, self.to_left = {"x": self.right}, {"x": self.left}
        self.peers = [(dz, dy) for dz in range(8) for dy in range(2) if dz or dy]

    def peer(self, dz, dy):
        there = {"z": lax.rem(self.z + dz, 8)}
        if dy:
            there["y_hi"] = 1 - self.y_hi
        return there


def score_steps(at, send, dosage, pheno, weight_rows, part, every, scratch):
    coded, codes, placed, cols_in, turned, near_w, a, p, s, n, f, own_sem = scratch
    snps, own = dosage.shape
    samples, cols = cols_in.shape
    nulls = codes.shape[0] // 2
    copies = nulls + 1
    mine = span(at.me, own)
    coming = [
        send(coded.at[:, mine], coded.at[:, mine], a, i, there)
        for i, there in enumerate((at.near, at.cross, at.sibling))
    ]
    half = own // 2
    pheno_coming = []
    for i, (there, target, h) in enumerate(
        (
            (at.near, at.near_id, 0), (at.cross, at.cross_id, 0),
            (at.far, at.near_id, 1), (at.far_cross, at.cross_id, 1),
        )
    ):
        pheno_coming.append(
            send(
                pheno.at[pl.ds(h * half, half), span(target, cols)],
                cols_in.at[pl.ds(pl.multiple_of(at.me * own + h * half, half), half)],
                p, i, there,
            )
        )
    pheno_coming.append(
        send(pheno.at[:, span(at.sib_id, cols)], cols_in.at[mine], p, 4, at.sibling)
    )
    stay = pltpu.make_async_copy(pheno.at[:, span(at.me, cols)], cols_in.at[mine], own_sem)
    stay.start()
    placed[:LEAD, :] = jnp.ones((LEAD, samples), BF16)
    for owner in range(4):
        every[owner, copies * snps :] = jnp.zeros((every.shape[1] - copies * snps, cols), BF16)
    for copy in coming:
        copy.wait_recv()

    codes[...] = coded[snps:, :].astype(F32)
    dose = coded[:snps, :]
    placed[LEAD : LEAD + snps, :] = dose
    dose32 = dose.astype(F32)
    dose_mean = jnp.sum(dose32, axis=1, keepdims=True) / samples
    dose_square = jnp.sum(dose32 * dose32, axis=1, keepdims=True) / samples
    spread_rows = jnp.sqrt(samples * (dose_square + 1e-05))
    steps = samples // LOW

    @pl.loop(0, nulls)
    def _(k):
        high = codes[pl.ds(k, 1), :]
        low = codes[pl.ds(nulls + k, 1), :]
        values = coded[:snps, :]
        masked = jnp.concatenate(
            [values * (high == F32(h)).astype(F32).astype(BF16) for h in range(steps)], axis=0
        )
        ids = lax.broadcasted_iota(jnp.int32, (LOW, samples), 0).astype(F32)
        onehot = (ids == low).astype(F32).astype(BF16)
        got = lax.dot_general(masked, onehot, NT, preferred_element_type=F32).astype(BF16)
        rows = pl.ds(pl.multiple_of(LEAD + (k + 1) * snps, 16), snps)
        for h in range(steps):
            placed[rows, h * LOW : (h + 1) * LOW] = got[h * snps : (h + 1) * snps]

    stay.wait()
    for copy in pheno_coming:
        copy.wait_recv()

    per = copies // CHUNKS
    total = None
    to_sib, to_near = [], []
    for c in range(CHUNKS):
        first = 0 if c == 0 else LEAD + c * per * snps
        last = LEAD + (c + 1) * per * snps
        raw = jnp.dot(placed[first:last, :], cols_in[...], preferred_element_type=F32)
        if c == 0:
            total = raw[:1]
            raw = raw[LEAD:]
        for j in range(per):
            value = (raw[j * snps : (j + 1) * snps] - dose_mean * total) / spread_rows
            row = (c * per + j) * snps
            every[at.me, row : row + snps] = value.astype(BF16)
        block = every.at[at.me, pl.ds(c * per * snps, per * snps)]
        to_near.append(send(block, block, n, c, at.near))
        to_sib.append(send(block, block, s, c, at.sibling))

    end = copies * snps
    turned[...] = every[at.me, snps:end].astype(F32).T.astype(BF16)
    passed = []
    for c in range(CHUNKS):
        to_near[c].wait_recv()
        block = every.at[at.near_id, pl.ds(c * per * snps, per * snps)]
        passed.append(send(block, block, f, c, at.sibling))
    for copy in to_sib + passed:
        copy.wait_recv()
    for r in range(3):
        value = every[lax.rem(at.me + r, 4), snps:end].astype(F32) * weight_rows[...]
        near_w[:, r * cols : (r + 1) * cols] = value.astype(BF16)
    for i in range(2):
        for h in range(2):
            row, first = (i * 2 + h) * TILE, i * TILE + h * WIDE
            part[row : row + TILE, :] = jnp.dot(
                turned[i * TILE : (i + 1) * TILE, :], near_w[:, first : first + WIDE],
                preferred_element_type=F32,
            ).astype(BF16)


def spread_steps(at, send, total, part, gram, scratch):
    x_slots, pair, acc, slots, chunk, xr, rr, gr, xg, ys, cs = scratch
    rows = part.shape[0]
    block, half, bit = rows // 4, rows // 8, rows // 64
    x, z, y_hi = at.x, at.z, at.y_hi
    right, left, across = at.right, at.left, at.across

    def half_of(owner, h):
        return part.at[pl.ds(pl.multiple_of(owner * block + h * half, half), half)]

    def x_sent(i, src, there):
        return send(src, x_slots.at[i], xr, i, there)

    hop_r = x_sent(0, half_of(across, 0), at.to_right)
    hop_l = x_sent(1, half_of(across, 1), at.to_left)
    own_r = x_sent(2, half_of(right, 1), at.to_right)
    own_l = x_sent(3, half_of(left, 0), at.to_left)

    def added(dst, sources):
        @pl.loop(0, half, step=32)
        def _(r):
            rows_at = pl.ds(pl.multiple_of(r, 32), 32)
            value = sources[0][rows_at, :].astype(F32)
            for source in sources[1:]:
                value += source[rows_at, :].astype(F32)
            dst[rows_at, :] = value.astype(BF16)

    hop_r.wait_recv()
    added(pair.at[0], [half_of(right, 0), x_slots.at[0]])
    sum_r = x_sent(4, pair.at[0], at.to_right)
    hop_l.wait_recv()
    added(pair.at[1], [half_of(left, 1), x_slots.at[1]])
    sum_l = x_sent(5, pair.at[1], at.to_left)
    own_l.wait_recv()
    sum_r.wait_recv()
    added(acc.at[pl.ds(0, half)], [half_of(x, 0), x_slots.at[3], x_slots.at[4]])
    own_r.wait_recv()
    sum_l.wait_recv()
    added(acc.at[pl.ds(half, half)], [half_of(x, 1), x_slots.at[2], x_slots.at[5]])

    def bit_at(at_y, at_z):
        return pl.ds(pl.multiple_of((at_y * 8 + at_z) * bit, bit), bit)

    arrive = []
    for i, (dz, dy) in enumerate(at.peers):
        at_y = 1 - y_hi if dy else y_hi
        src = acc.at[bit_at(at_y, lax.rem(z + dz, 8))]
        arrive.append(send(src, slots.at[i], rr, i, at.peer(dz, dy)))
    value = acc[bit_at(y_hi, z), :].astype(F32)
    for i, copy in enumerate(arrive):
        copy.wait_recv()
        value += slots[i].astype(F32)
    chunk[...] = (value / total).astype(BF16)

    piece = at.me
    mine = pl.ds(pl.multiple_of(x * block + (y_hi * 8 + z) * bit, bit), bit)
    arrive = []
    for i, (dz, dy) in enumerate(at.peers):
        arrive.append(send(chunk, gram.at[piece, mine], gr, i, at.peer(dz, dy)))
    gram[piece, mine] = chunk[...]
    for copy in arrive:
        copy.wait_recv()

    def at_half(which, owner, h):
        return gram.at[which, pl.ds(pl.multiple_of(owner * block + h * half, half), half)]

    def at_block(which, owner):
        return gram.at[which, span(owner, block)]

    def passed(src, sems, i, there):
        return send(src, src, sems, i, there)

    def to_y(i, owner):
        return (
            passed(at_half(piece, owner, 0), ys, 2 * i, at.near),
            passed(at_half(piece, owner, 1), ys, 2 * i + 1, at.far),
        )

    go_r = passed(at_block(piece, x), xg, 0, at.to_right)
    go_l = passed(at_block(piece, x), xg, 1, at.to_left)
    y_own = to_y(0, x)
    c_all = [passed(at_block(piece, x), cs, 0, at.sibling)]
    go_r.wait_recv()
    hop_r = passed(at_half(piece, left, 0), xg, 2, at.to_right)
    y_left = to_y(1, left)
    go_l.wait_recv()
    hop_l = passed(at_half(piece, right, 1), xg, 3, at.to_left)
    y_right = to_y(2, right)
    c_all.append(passed(at_block(piece, left), cs, 1, at.sibling))
    c_all.append(passed(at_block(piece, right), cs, 2, at.sibling))

    def from_y(copies, owner, i):
        for copy in copies:
            copy.wait_recv()
        c_all.append(passed(at_block(at.near_id, owner), cs, i, at.sibling))

    from_y(y_own, x, 3)
    hop_r.wait_recv()
    y_far = [passed(at_half(piece, across, 0), ys, 6, at.near)]
    hop_l.wait_recv()
    y_far.append(passed(at_half(piece, across, 1), ys, 7, at.far))
    c_all.append(passed(at_block(piece, across), cs, 4, at.sibling))
    from_y(y_left, left, 5)
    from_y(y_right, right, 6)
    from_y(y_far, across, 7)
    for copy in c_all:
        copy.wait_recv()


def white_steps(at, send, genes, gram, every, out, scratch):
    lower, start, first, second, leaving, os = scratch
    cols = every.shape[2]
    share = leaving.shape[1]
    pieces = 4
    tall = pieces * 2 * TILE

    def keep(dst, index, value):
        dst[span(index, TILE), :] = value
        dst[pl.ds(pl.multiple_of(tall + index * TILE, TILE), TILE), :] = value

    mine = span(at.me, share)
    for b in range(pieces):
        block = every[b, mine].astype(F32)
        block = jnp.concatenate([block, jnp.zeros((LANES - share, cols), F32)], axis=0)
        block = block.T.astype(BF16)
        for i in range(2):
            keep(start, 2 * b + i, block[i * TILE : (i + 1) * TILE])

    def strip(a, i, h):
        return gram[a, (i * 2 + h) * TILE : (i * 2 + h + 1) * TILE, :]

    spot = lax.broadcasted_iota(jnp.int32, (TILE, TILE), 0)
    spot = spot == lax.broadcasted_iota(jnp.int32, (TILE, TILE), 1)
    trace = F32(0)
    for a in range(pieces):
        for i in range(2):
            tile = strip(a, i, 0)[:, :TILE].astype(F32)
            trace += jnp.sum(jnp.where(spot, tile, F32(0)))
    scale = jnp.full((1, LANES), trace / genes + 1e-06, F32)
    inverse = 1.0 / scale
    rsqrt = 1.0 / jnp.sqrt(scale)

    @pl.loop(0, pieces)
    def _(a):
        for i in range(2):
            one, two, three = (lax.rem(2 * a + i + d, 8) for d in (1, 2, 3))
            flip = strip(a, i, 0)[:, TILE:].astype(F32).T.astype(BF16)
            lower[one, :, 2 * TILE :] = flip[:TILE]
            lower[two, : TILE // 2, TILE : 2 * TILE] = flip[TILE:]
            flip = strip(a, i, 1)[:, : WIDE - TILE].astype(F32).T.astype(BF16)
            lower[two, TILE // 2 :, TILE : 2 * TILE] = flip[: TILE // 2]
            lower[three, :, :TILE] = flip[TILE // 2 :]

    def image(left, a, i):
        j = 2 * a + i
        base = lax.rem(j + 5, 8) * TILE

        def rows(offset, size):
            return left[pl.ds(pl.multiple_of(base + offset, LANES), size), :]

        value = jnp.dot(lower[j], rows(0, 3 * TILE), preferred_element_type=F32)
        value += jnp.dot(strip(a, i, 0), rows(3 * TILE, WIDE), preferred_element_type=F32)
        value += jnp.dot(strip(a, i, 1), rows(3 * TILE + WIDE, WIDE), preferred_element_type=F32)
        return value * inverse

    def own(source, a, i):
        return source[span(2 * a + i, TILE), :].astype(F32)

    @pl.loop(0, pieces)
    def _(a):
        for i in range(2):
            keep(first, 2 * a + i, (1.5 * own(start, a, i) - 0.5 * image(start, a, i)).astype(BF16))

    @pl.loop(0, pieces)
    def _(a):
        for i in range(2):
            keep(second, 2 * a + i, image(first, a, i).astype(BF16))

    @pl.loop(0, pieces)
    def _(a):
        for i in range(2):
            inner = 1.5 * own(second, a, i) - 0.5 * image(second, a, i)
            keep(first, 2 * a + i, (1.5 * own(start, a, i) - 0.5 * inner).astype(BF16))

    coming = []
    targets = ((at.near_id, at.near), (at.cross_id, at.cross), (at.sib_id, at.sibling))
    for t, (a, there) in enumerate((*targets, (at.me, None))):
        for i in range(2):
            value = (1.5 * own(first, a, i) - 0.5 * image(first, a, i)) * rsqrt
            value = value.T[:share].astype(BF16)
            cols_at = slice(i * TILE, (i + 1) * TILE)
            if there is None:
                out[mine, cols_at] = value
            else:
                leaving[t, :, cols_at] = value
        if there is not None:
            coming.append(send(leaving.at[t], out.at[mine], os, t, there))
    for copy in coming:
        copy.wait_recv()


def kernel(sizes, total, dosage, pheno, perm, weight_rows, out, *scratch):
    refs, position = [], 0
    for size in sizes:
        refs.append(scratch[position : position + size])
        position += size
    plain, pairs, own_sem = refs
    pairs = [(pairs[i], pairs[i + 1]) for i in range(0, len(pairs), 2)]
    (
        coded, codes, placed, cols_in, turned, near_w, part, every,
        x_slots, pair, acc, slots, chunk, gram, lower, start, first, second, leaving,
    ) = plain
    at, send = Place(), Sender()
    barrier = pltpu.get_barrier_semaphore()
    greeted = [at.sibling, at.near, at.cross, at.far, at.far_cross, at.to_right, at.to_left]
    greeted += [at.peer(*p) for p in at.peers]
    for there in greeted:
        pl.semaphore_signal(barrier, inc=1, device_id=there, device_id_type=MESH)
    snps, own = dosage.shape
    mine = span(at.me, own)
    coded[:snps, mine] = dosage[...].astype(F32).astype(BF16)
    source = perm[...]
    both = jnp.concatenate([lax.shift_right_logical(source, 8), source & 255], axis=0)
    coded[snps:, mine] = both.astype(F32).astype(BF16)
    pl.semaphore_wait(barrier, len(greeted))
    score_steps(
        at, send, dosage, pheno, weight_rows, part, every,
        (coded, codes, placed, cols_in, turned, near_w, *pairs[:5], own_sem[0]),
    )
    spread_steps(at, send, total, part, gram, (x_slots, pair, acc, slots, chunk, *pairs[5:11]))
    white_steps(
        at, send, pheno.shape[1], gram, every, out,
        (lower, start, first, second, leaving, pairs[11]),
    )
    send.finish()


def shards(dosage, pheno, perm, snp_weight):
    snps, own = dosage.shape
    genes = pheno.shape[1]
    groups = lax.axis_size(SAMP)
    nulls = perm.shape[0]
    copies = nulls + 1
    rows = copies * snps
    cols = genes // groups
    samples = own * groups
    share = -(-rows // (16 * groups)) * 16
    tall = 4 * TILE
    weight_rows = jnp.tile(snp_weight, nulls)[:, None]
    dma = pltpu.SemaphoreType.DMA
    vmem = pl.BlockSpec(memory_space=pltpu.VMEM)
    plain = [
        pltpu.VMEM((snps + 2 * nulls, samples), BF16),
        pltpu.VMEM((2 * nulls, samples), F32),
        pltpu.VMEM((LEAD + rows, samples), BF16),
        pltpu.VMEM((samples, cols), BF16),
        pltpu.VMEM((cols, rows - snps), BF16),
        pltpu.VMEM((rows - snps, 3 * cols), BF16),
        pltpu.VMEM((tall, WIDE), BF16),
        pltpu.VMEM((groups, share * groups, cols), BF16),
        pltpu.VMEM((6, tall // 8, WIDE), BF16),
        pltpu.VMEM((2, tall // 8, WIDE), BF16),
        pltpu.VMEM((tall // 4, WIDE), BF16),
        pltpu.VMEM((15, tall // 64, WIDE), BF16),
        pltpu.VMEM((tall // 64, WIDE), BF16),
        pltpu.VMEM((groups, tall, WIDE), BF16),
        pltpu.VMEM((genes // TILE, TILE, 3 * TILE), BF16),
        *[pltpu.VMEM((2 * genes, LANES), BF16)] * 3,
        pltpu.VMEM((3, share, cols), BF16),
    ]
    counts = [3, 5, 3, 3, 3, 6, 15, 15, 4, 8, 8, 3]
    pairs = [dma((n,)) for n in counts for _ in range(2)]
    sizes = (len(plain), len(pairs), 1)
    white = pl.pallas_call(
        functools.partial(kernel, sizes, nulls * snps * lax.axis_size(SNP)),
        out_shape=jax.ShapeDtypeStruct((share * groups, cols), BF16),
        in_specs=[vmem, pl.BlockSpec(memory_space=pl.ANY), vmem, vmem],
        out_specs=vmem,
        scratch_shapes=[*plain, *pairs, dma],
        compiler_params=pltpu.CompilerParams(
            collective_id=0, has_side_effects=True, vmem_limit_bytes=48 << 20
        ),
        name="whitened_scores",
    )(dosage, pheno, perm, weight_rows)
    return white[:rows].reshape(copies, snps, cols)


def solution(mesh):
    finer = Mesh(mesh.devices.reshape(2, 2, 4, 8, 2), (*SAMP, *SNP))
    in_specs = (P(SNP, SAMP), P(SAMP, None), P(None, SAMP), P(SNP))
    return jax.shard_map(
        shards, mesh=finer, in_specs=in_specs, out_specs=P(None, SNP, SAMP), check_vma=False
    )
```

time: 371 us -> 116 us (0.31)
  waiting for transfers between devices: 113 us -> 0 us
  Pallas kernels: 0 us -> 111 us
  blocking collectives: 109 us -> 0 us
  local copies, waits for them, and re-layouts: 61.6 us -> 4.76 us
  matrix products: 43.9 us -> 0 us
  starting transfers between devices: 28.6 us -> 0 us
  other arithmetic: 9.98 us -> 0 us
    all_to_all x4 -> x0, waiting for transfers between devices: 113 us -> none  [sent_parts(): return lax.all_to_all(array, axis, split_axis=0, concat_axis=0, tiled=True)]
    pallas_call x0 -> x1, Pallas kernels: none -> 111 us  [shards(): pl.pallas_call(functools.partial(kernel, sizes, nulls * snps * lax.axis_s...]
    all_to_all x7 -> x0, blocking collectives: 109 us -> none  [sent_parts(): return lax.all_to_all(array, axis, split_axis=0, concat_axis=0, tiled=True)]
    dot_general x26 -> x0, matrix products: 43.9 us -> none  [the longest x16 32.9 us: image(): jnp.dot(left, gram[a], preferred_element_type=F32)]
    unnamed x88 -> x6, local copies, waits for them, and re-layouts: 44.5 us -> 3.2 us
    all_to_all x4 -> x0, starting transfers between devices: 28.6 us -> none  [sent_parts(): return lax.all_to_all(array, axis, split_axis=0, concat_axis=0, tiled=True)]
    broadcast_in_dim x6 -> x0, local copies, waits for them, and re-layouts: 6.17 us -> none  [copies_from(): jnp.broadcast_to(array[None], (devices, *array.shape))]
    reduce_sum x6 -> x0, other arithmetic: 5.08 us -> none  [the longest x3 2.31 us: summed_share(): return jnp.sum(arrived.astype(F32), axis=0)]
  transfers between devices with their start and end apart: 4 -> 0, of which waited for: 3 -> 0; matrix products, arithmetic and copies ran while one was open for 15% -> 0% of each run, Pallas kernels for 0% -> 0%
where the time goes in v4:
time: 116 us
  Pallas kernels  111 us (96%)
  local copies, waits for them, and re-layouts  4.76 us (4%)
    pallas_call x1, Pallas kernels, shards(): pl.pallas_call(functools.partial(kernel, sizes, nulls * snps * lax.axis_s...  111 us
    unnamed x6, local copies, waits for them, and re-layouts  3.2 us

profile of v4, /device:TPU:1, one launch (start us, length us, event | category | flops | bytes accessed | tf_op | source)
XLA Modules:
  0.0 115.6 jit_solution(11884514971356602515)
XLA Ops:
  0.0 0.7 tile.2
  0.7 0.1 broadcast_in_dim_tile.4.weight_rows
  0.8 0.0 copy-start
  0.8 1.6 %copy-done = bf16[512,2048]{1,0:T(8,128)(2,1)S(1)} copy-done((bf16[512,2048]{1,0:T(8,128)(2,1)S(1)}, bf16[512,2048]{1,0:T(8,128)(2,1)}, u32[]{:S(2)}) %copy-start) | copy-done | bytes 2097176
  2.4 0.0 copy-start.1
  2.4 0.9 copy-done.1
  3.3 0.0 copy-start.2
  3.3 0.7 copy-done.2
  4.0 110.8 %whitened_scores.1 = bf16[448,512]{1,0:T(8,128)(2,1)S(1)} custom-call(s32[48,512]{1,0:T(8,128)S(1)} %copy-done.1, bf16[512,2048]{1,0:T(8,128)(2,1)S(1)} %copy-done, s32[8,512]{1,0:T(8,128)S(1)} %copy-done.2, f32[384,1]{1,0:T(8,128)S(1)} %broadcast_in_dim_tile.4.weight_rows), custom_call_target="tpu_custom_call" | custom-call | tf_op jit(solution)/shard_map/whitened_scores/pallas_call | solution.py:450
  114.8 0.8 slice.3
Async XLA Ops:
  0.8 1.6 %copy-start = (bf16[512,2048]{1,0:T(8,128)(2,1)S(1)}, bf16[512,2048]{1,0:T(8,128)(2,1)}, u32[]{:S(2)}) copy-start(bf16[512,2048]{1,0:T(8,128)(2,1)} %pheno.1) | copy-start | bytes 6291460
  2.4 0.9 copy-start.1
  3.3 0.7 copy-start.2

commit v5 on v4

v5 whole, which is shorter than its diff:
```python
import functools

import jax
import jax.numpy as jnp
from jax import lax
from jax.experimental import pallas as pl
from jax.experimental.pallas import tpu as pltpu
from jax.sharding import Mesh
from jax.sharding import PartitionSpec as P

SAMP = ("y_lo", "core")
SNP = ("x", "z", "y_hi")
F32 = jnp.float32
BF16 = jnp.bfloat16
NT = (((1,), (1,)), ((), ()))
LOW = 256
TILE = 256
LANES = 128
LEAD = 16
CHUNKS = 3
CUTS = ((0, 6), (6, 4))
MESH = pl.DeviceIdType.MESH


def span(index, size):
    return pl.ds(pl.multiple_of(index * size, size), size)


class Sender:
    def __init__(self):
        self.started = []

    def __call__(self, src, dst, sems, i, there):
        copy = pltpu.make_async_remote_copy(
            src_ref=src, dst_ref=dst, send_sem=sems[0].at[i], recv_sem=sems[1].at[i],
            device_id=there, device_id_type=MESH,
        )
        copy.start()
        self.started.append(copy)
        return copy

    def finish(self):
        for copy in self.started:
            copy.wait_send()


class Place:
    def __init__(self):
        x, z, y_hi = lax.axis_index("x"), lax.axis_index("z"), lax.axis_index("y_hi")
        y_lo, core = lax.axis_index("y_lo"), lax.axis_index("core")
        self.x, self.z, self.y_hi, self.y_lo, self.core = x, z, y_hi, y_lo, core
        self.me = y_lo * 2 + core
        self.sib_id = y_lo * 2 + 1 - core
        self.near_id = (1 - y_lo) * 2 + core
        self.cross_id = (1 - y_lo) * 2 + 1 - core
        self.sibling = {"core": 1 - core}
        self.near = {"y_lo": 1 - y_lo}
        self.cross = {"y_lo": 1 - y_lo, "core": 1 - core}
        self.far = {"y_lo": 1 - y_lo, "y_hi": 1 - y_hi}
        self.far_cross = {"y_lo": 1 - y_lo, "y_hi": 1 - y_hi, "core": 1 - core}
        self.right, self.left = lax.rem(x + 1, 4), lax.rem(x + 3, 4)
        self.across = lax.rem(x + 2, 4)
        self.to_right, self.to_left = {"x": self.right}, {"x": self.left}
        self.peers = [(dz, dy) for dz in range(8) for dy in range(2) if dz or dy]

    def peer(self, dz, dy):
        there = {"z": lax.rem(self.z + dz, 8)}
        if dy:
            there["y_hi"] = 1 - self.y_hi
        return there


def score_steps(at, send, dosage, pheno, snp_weight, part, every, scratch):
    coded, codes, placed, cols_in, turned, near_w, a, p, s, n, f, own_sem = scratch
    snps, own = dosage.shape
    samples, cols = cols_in.shape
    nulls = codes.shape[0] // 2
    copies = nulls + 1
    mine = span(at.me, own)
    coming = [
        send(coded.at[:, mine], coded.at[:, mine], a, i, there)
        for i, there in enumerate((at.near, at.cross, at.sibling))
    ]
    cut = own * 7 // 16
    pheno_coming = []
    for i, (there, target, first, size) in enumerate(
        (
            (at.near, at.near_id, 0, cut), (at.far, at.near_id, cut, own - cut),
            (at.cross, at.cross_id, 0, cut), (at.far_cross, at.cross_id, cut, own - cut),
        )
    ):
        pheno_coming.append(
            send(
                pheno.at[pl.ds(first, size), span(target, cols)],
                cols_in.at[pl.ds(pl.multiple_of(at.me * own + first, 32), size)],
                p, i, there,
            )
        )
    pheno_coming.append(
        send(pheno.at[:, span(at.sib_id, cols)], cols_in.at[mine], p, 4, at.sibling)
    )
    stay = pltpu.make_async_copy(pheno.at[:, span(at.me, cols)], cols_in.at[mine], own_sem)
    stay.start()
    placed[:LEAD, :] = jnp.ones((LEAD, samples), BF16)
    for owner in range(4):
        every[owner, copies * snps :] = jnp.zeros((every.shape[1] - copies * snps, cols), BF16)
    for copy in coming:
        copy.wait_recv()

    codes[...] = coded[snps:, :].astype(F32)
    dose = coded[:snps, :]
    placed[LEAD : LEAD + snps, :] = dose
    dose32 = dose.astype(F32)
    dose_mean = jnp.sum(dose32, axis=1, keepdims=True) / samples
    dose_square = jnp.sum(dose32 * dose32, axis=1, keepdims=True) / samples
    spread_rows = jnp.sqrt(samples * (dose_square + 1e-05))
    steps = samples // LOW

    @pl.loop(0, nulls)
    def _(k):
        high = codes[pl.ds(k, 1), :]
        low = codes[pl.ds(nulls + k, 1), :]
        values = coded[:snps, :]
        masked = jnp.concatenate(
            [values * (high == F32(h)).astype(F32).astype(BF16) for h in range(steps)], axis=0
        )
        ids = lax.broadcasted_iota(jnp.int32, (LOW, samples), 0).astype(F32)
        onehot = (ids == low).astype(F32).astype(BF16)
        got = lax.dot_general(masked, onehot, NT, preferred_element_type=F32).astype(BF16)
        rows = pl.ds(pl.multiple_of(LEAD + (k + 1) * snps, 16), snps)
        for h in range(steps):
            placed[rows, h * LOW : (h + 1) * LOW] = got[h * snps : (h + 1) * snps]

    stay.wait()
    for copy in pheno_coming:
        copy.wait_recv()

    per = copies // CHUNKS
    total = None
    to_sib, to_near = [], []
    for c in range(CHUNKS):
        first = 0 if c == 0 else LEAD + c * per * snps
        last = LEAD + (c + 1) * per * snps
        raw = jnp.dot(placed[first:last, :], cols_in[...], preferred_element_type=F32)
        if c == 0:
            total = raw[:1]
            raw = raw[LEAD:]
        for j in range(per):
            value = (raw[j * snps : (j + 1) * snps] - dose_mean * total) / spread_rows
            row = (c * per + j) * snps
            every[at.me, row : row + snps] = value.astype(BF16)
        block = every.at[at.me, pl.ds(c * per * snps, per * snps)]
        to_near.append(send(block, block, n, c, at.near))
        to_sib.append(send(block, block, s, c, at.sibling))

    end = copies * snps
    turned[...] = every[at.me, snps:end].astype(F32).T.astype(BF16)
    spot = lax.broadcasted_iota(jnp.int32, (snps, snps), 0)
    spot = spot == lax.broadcasted_iota(jnp.int32, (snps, snps), 1)
    weight = jnp.sum(jnp.where(spot, snp_weight[...], F32(0)), axis=1, keepdims=True)

    def weigh(r, which):
        for k in range(nulls):
            value = every[which, (k + 1) * snps : (k + 2) * snps].astype(F32) * weight
            near_w[k * snps : (k + 1) * snps, r * cols : (r + 1) * cols] = value.astype(BF16)

    def tile(row, i, first):
        got = jnp.dot(
            turned[i * TILE : (i + 1) * TILE, :],
            near_w[:, pl.ds(pl.multiple_of(first, TILE), TILE)], preferred_element_type=F32,
        )
        got = got.astype(BF16)
        for h in range(2):
            at_row = (2 * row + h) * TILE
            part[at_row : at_row + TILE, :] = got[:, h * LANES : (h + 1) * LANES]

    weigh(0, at.me)
    for copy in to_sib:
        copy.wait_recv()
    weigh(1, at.sib_id)
    for i in range(2):
        for t in range(2):
            tile(i * 3 + t, i, t * TILE)
        tile(i * 3 + 2, i, cols + lax.rem(i + at.core, 2) * TILE)
    yield
    passed = []

    def hand_on(c):
        to_near[c].wait_recv()
        block = every.at[at.near_id, pl.ds(c * per * snps, per * snps)]
        passed.append(send(block, block, f, c, at.sibling))

    hand_on(0)
    hand_on(1)
    yield
    hand_on(2)
    yield
    for copy in passed:
        copy.wait_recv()
    weigh(2, (1 - at.y_lo) * 2 + lax.rem(at.core + at.y_lo, 2))
    for i in range(2):
        for t in range(2):
            tile(6 + i * 2 + t, i, 2 * cols + t * TILE)
    yield


def spread_chunk(at, send, total, part, gram, scratch, k):
    x_slots, pair, acc, slots, chunk, xr, rr, gr, xg, ys, cs, own_in, own_out = scratch
    base, rows = (n * 2 * TILE for n in CUTS[k])
    block, half, bit = rows // 4, rows // 8, rows // 64
    x, z, y_hi = at.x, at.z, at.y_hi
    right, left, across = at.right, at.left, at.across
    x_slots, pair, acc = x_slots.at[k], pair.at[k], acc.at[k]
    slots, chunk = slots.at[k], chunk.at[k, pl.ds(0, bit)]

    def half_of(owner, h):
        return part.at[pl.ds(pl.multiple_of(base + owner * block + h * half, 64), half)]

    def slot(i):
        return x_slots.at[i, pl.ds(0, half)]

    def x_sent(i, src, there):
        return send(src, slot(i), xr, 6 * k + i, there)

    def added(dst, sources):
        @pl.loop(0, half, step=64)
        def _(r):
            rows_at = pl.ds(pl.multiple_of(r, 64), 64)
            value = sources[0][rows_at, :].astype(F32)
            for source in sources[1:]:
                value += source[rows_at, :].astype(F32)
            dst[rows_at, :] = value.astype(BF16)

    def summed(h):
        return pair.at[h, pl.ds(0, half)]

    hop_r = x_sent(0, half_of(across, 0), at.to_right)
    hop_l = x_sent(1, half_of(across, 1), at.to_left)
    own_r = x_sent(2, half_of(right, 1), at.to_right)
    own_l = x_sent(3, half_of(left, 0), at.to_left)
    yield
    hop_r.wait_recv()
    added(summed(0), [half_of(right, 0), slot(0)])
    sum_r = x_sent(4, summed(0), at.to_right)
    hop_l.wait_recv()
    added(summed(1), [half_of(left, 1), slot(1)])
    sum_l = x_sent(5, summed(1), at.to_left)
    yield
    own_l.wait_recv()
    sum_r.wait_recv()
    added(acc.at[pl.ds(0, half)], [half_of(x, 0), slot(3), slot(4)])
    own_r.wait_recv()
    sum_l.wait_recv()
    added(acc.at[pl.ds(half, half)], [half_of(x, 1), slot(2), slot(5)])

    def bit_at(at_y, at_z):
        return acc.at[pl.ds(pl.multiple_of((at_y * 8 + at_z) * bit, 16), bit)]

    arrive = []
    for i, (dz, dy) in enumerate(at.peers):
        at_y = 1 - y_hi if dy else y_hi
        src = bit_at(at_y, lax.rem(z + dz, 8))
        dst = slots.at[i, pl.ds(0, bit)]
        arrive.append(send(src, dst, rr, 15 * k + i, at.peer(dz, dy)))
    stay = pltpu.make_async_copy(bit_at(y_hi, z), slots.at[15, pl.ds(0, bit)], own_in.at[k])
    stay.start()
    yield
    stay.wait()
    value = slots[15, :bit].astype(F32)
    for i, copy in enumerate(arrive):
        copy.wait_recv()
        value += slots[i, :bit].astype(F32)
    chunk[...] = (value / total).astype(BF16)

    piece = at.me
    first = base + x * block + (y_hi * 8 + z) * bit
    dst = gram.at[piece, pl.ds(pl.multiple_of(first, 16), bit)]
    arrive = []
    for i, (dz, dy) in enumerate(at.peers):
        arrive.append(send(chunk, dst, gr, 15 * k + i, at.peer(dz, dy)))
    stay = pltpu.make_async_copy(chunk, dst, own_out.at[k])
    stay.start()
    yield
    stay.wait()
    for copy in arrive:
        copy.wait_recv()

    def at_half(which, owner, h):
        return gram.at[which, pl.ds(pl.multiple_of(base + owner * block + h * half, 64), half)]

    def at_block(which, owner):
        return gram.at[which, pl.ds(pl.multiple_of(base + owner * block, 128), block)]

    def to_x(i, src, there):
        return send(src, src, xg, 4 * k + i, there)

    c_all = []

    def to_sibling(which, owner):
        src = at_block(which, owner)
        c_all.append(send(src, src, cs, 8 * k + len(c_all), at.sibling))

    def to_y(i, owner, h):
        src = at_half(piece, owner, h)
        return send(src, src, ys, 8 * k + 2 * i + h, at.far if h else at.near)

    go_r = to_x(0, at_block(piece, x), at.to_right)
    go_l = to_x(1, at_block(piece, x), at.to_left)
    y_own = [to_y(0, x, h) for h in range(2)]
    to_sibling(piece, x)
    yield
    go_r.wait_recv()
    hop_r = to_x(2, at_half(piece, left, 0), at.to_right)
    y_left = [to_y(1, left, h) for h in range(2)]
    go_l.wait_recv()
    hop_l = to_x(3, at_half(piece, right, 1), at.to_left)
    y_right = [to_y(2, right, h) for h in range(2)]
    to_sibling(piece, left)
    to_sibling(piece, right)

    def from_y(copies, owner):
        for copy in copies:
            copy.wait_recv()
        to_sibling(at.near_id, owner)

    yield
    hop_r.wait_recv()
    y_far = [to_y(3, across, 0)]
    hop_l.wait_recv()
    y_far.append(to_y(3, across, 1))
    to_sibling(piece, across)
    from_y(y_own, x)
    yield
    from_y(y_left, left)
    from_y(y_right, right)
    yield
    from_y(y_far, across)
    yield
    for copy in c_all:
        copy.wait_recv()


def white_steps(at, send, genes, gram, every, out, scratch):
    lower, start, first, second, partial, leaving, os = scratch
    cols = every.shape[2]
    share = leaving.shape[1]
    pieces = 4

    mine = span(at.me, share)
    for b in range(pieces):
        block = every[b, mine].astype(F32)
        block = jnp.concatenate([block, jnp.zeros((LANES - share, cols), F32)], axis=0)
        start[b * cols : (b + 1) * cols, :] = block.T.astype(BF16)
    yield

    def strip(a, row):
        first, last = 2 * row * TILE, 2 * (row + 1) * TILE
        halves = gram[a, first : first + TILE, :], gram[a, first + TILE : last, :]
        return jnp.concatenate(halves, axis=1)

    def flipped(a, row):
        return strip(a, row).astype(F32).T.astype(BF16)

    def product(tile, left, j):
        return jnp.dot(tile, left[span(j, TILE), :], preferred_element_type=F32)

    def places(a, i):
        c, y = lax.rem(a, 2), a // 2
        pair = 2 * (2 * y + 1 - c) + lax.rem(i + c, 2)
        rest = 2 * (2 * y + 1 - c) + 1 - lax.rem(i + c, 2)
        direct = 2 * (1 - y) + lax.rem(c + y, 2)
        turned = 2 * (1 - y) + 1 - lax.rem(c + y, 2)
        return pair, rest, direct, turned

    spot = lax.broadcasted_iota(jnp.int32, (TILE, TILE), 0)
    spot = spot == lax.broadcasted_iota(jnp.int32, (TILE, TILE), 1)
    trace = F32(0)
    for a in range(pieces):
        for i in range(2):
            trace += jnp.sum(jnp.where(spot, strip(a, i * 3 + i).astype(F32), F32(0)))
    scale = jnp.full((1, LANES), trace / genes + 1e-06, F32)
    inverse = 1.0 / scale
    rsqrt = 1.0 / jnp.sqrt(scale)

    @pl.loop(0, pieces)
    def _(a):
        for i in range(2):
            lower[places(a, i)[0], :, :TILE] = flipped(a, i * 3 + 2)

    def on_chip(left, a, i):
        pair, rest, _, _ = places(a, i)
        value = product(strip(a, i * 3), left, 2 * a)
        value += product(strip(a, i * 3 + 1), left, 2 * a + 1)
        value += product(strip(a, i * 3 + 2), left, pair)
        return value + product(lower[2 * a + i, :, :TILE], left, rest)

    def off_chip(left, a, i):
        _, _, direct, turned = places(a, i)
        value = None
        for t in range(2):
            one = product(strip(a, 6 + i * 2 + t), left, 2 * direct + t)
            one += product(lower[2 * a + i, :, (t + 1) * TILE : (t + 2) * TILE], left, 2 * turned + t)
            value = one if value is None else value + one
        return value

    def image(left, a, i):
        return (on_chip(left, a, i) + off_chip(left, a, i)) * inverse

    def own(source, a, i):
        return source[span(2 * a + i, TILE), :].astype(F32)

    @pl.loop(0, pieces)
    def _(a):
        for i in range(2):
            partial[span(2 * a + i, TILE), :] = on_chip(start, a, i)

    yield

    @pl.loop(0, pieces)
    def _(a):
        for i in range(2):
            direct = places(a, i)[2]
            for t in range(2):
                lower[2 * direct + t, :, (i + 1) * TILE : (i + 2) * TILE] = flipped(a, 6 + i * 2 + t)

    @pl.loop(0, pieces)
    def _(a):
        for i in range(2):
            value = (partial[span(2 * a + i, TILE), :] + off_chip(start, a, i)) * inverse
            first[span(2 * a + i, TILE), :] = (1.5 * own(start, a, i) - 0.5 * value).astype(BF16)

    @pl.loop(0, pieces)
    def _(a):
        for i in range(2):
            second[span(2 * a + i, TILE), :] = image(first, a, i).astype(BF16)

    @pl.loop(0, pieces)
    def _(a):
        for i in range(2):
            inner = 1.5 * own(second, a, i) - 0.5 * image(second, a, i)
            first[span(2 * a + i, TILE), :] = (1.5 * own(start, a, i) - 0.5 * inner).astype(BF16)

    coming = []
    targets = ((at.near_id, at.near), (at.cross_id, at.cross), (at.sib_id, at.sibling))
    for t, (a, there) in enumerate((*targets, (at.me, None))):
        for i in range(2):
            value = (1.5 * own(first, a, i) - 0.5 * image(first, a, i)) * rsqrt
            value = value.T[:share].astype(BF16)
            cols_at = slice(i * TILE, (i + 1) * TILE)
            if there is None:
                out[mine, cols_at] = value
            else:
                leaving[t, :, cols_at] = value
        if there is not None:
            coming.append(send(leaving.at[t], out.at[mine], os, t, there))
    for copy in coming:
        copy.wait_recv()
    yield


def kernel(sizes, total, dosage, pheno, perm, snp_weight, out, *scratch):
    refs, position = [], 0
    for size in sizes:
        refs.append(scratch[position : position + size])
        position += size
    plain, pairs, (singles,) = refs
    pairs = [(pairs[i], pairs[i + 1]) for i in range(0, len(pairs), 2)]
    (
        coded, codes, placed, cols_in, turned, near_w, part, every,
        x_slots, pair, acc, slots, chunk, gram, lower, start, first, second, partial, leaving,
        dose_here, perm_here,
    ) = plain
    at, send = Place(), Sender()
    barrier = pltpu.get_barrier_semaphore()
    greeted = [at.sibling, at.near, at.cross, at.far, at.far_cross, at.to_right, at.to_left]
    greeted += [at.peer(*p) for p in at.peers]
    for there in greeted:
        pl.semaphore_signal(barrier, inc=1, device_id=there, device_id_type=MESH)
    snps, own = dosage.shape
    mine = span(at.me, own)
    loads = [
        pltpu.make_async_copy(dosage, dose_here, singles.at[1]),
        pltpu.make_async_copy(perm, perm_here, singles.at[2]),
    ]
    for load in loads:
        load.start()
    for load in loads:
        load.wait()
    coded[:snps, mine] = dose_here[...].astype(F32).astype(BF16)
    source = perm_here[...]
    both = jnp.concatenate([lax.shift_right_logical(source, 8), source & 255], axis=0)
    coded[snps:, mine] = both.astype(F32).astype(BF16)
    pl.semaphore_wait(barrier, len(greeted))
    scores = score_steps(
        at, send, dosage, pheno, snp_weight, part, every,
        (coded, codes, placed, cols_in, turned, near_w, *pairs[:5], singles.at[0]),
    )
    moved = (
        x_slots, pair, acc, slots, chunk, *pairs[5:11], singles.at[pl.ds(3, 2)], singles.at[pl.ds(5, 2)],
    )
    here, cross = (spread_chunk(at, send, total, part, gram, moved, k) for k in range(2))
    white = white_steps(
        at, send, pheno.shape[1], gram, every, out,
        (lower, start, first, second, partial, leaving, pairs[11]),
    )
    for _ in range(3):
        next(scores)
        next(here)
    next(scores)
    next(cross)
    next(white)
    for _ in here:
        next(cross)
    next(white)
    for _ in cross:
        pass
    next(white)
    send.finish()


def shards(dosage, pheno, perm, snp_weight):
    snps, own = dosage.shape
    genes = pheno.shape[1]
    groups = lax.axis_size(SAMP)
    nulls = perm.shape[0]
    copies = nulls + 1
    rows = copies * snps
    cols = genes // groups
    samples = own * groups
    share = -(-rows // (16 * groups)) * 16
    tiles = 10
    most = max(n for _, n in CUTS) * 2 * TILE
    dma = pltpu.SemaphoreType.DMA
    vmem = pl.BlockSpec(memory_space=pltpu.VMEM)
    hbm = pl.BlockSpec(memory_space=pltpu.HBM)
    plain = [
        pltpu.VMEM((snps + 2 * nulls, samples), BF16),
        pltpu.VMEM((2 * nulls, samples), F32),
        pltpu.VMEM((LEAD + rows, samples), BF16),
        pltpu.VMEM((samples, cols), BF16),
        pltpu.VMEM((cols, rows - snps), BF16),
        pltpu.VMEM((rows - snps, 3 * cols), BF16),
        pltpu.VMEM((tiles * 2 * TILE, LANES), BF16),
        pltpu.VMEM((groups, share * groups, cols), BF16),
        pltpu.VMEM((2, 6, most // 8, LANES), BF16),
        pltpu.VMEM((2, 2, most // 8, LANES), BF16),
        pltpu.VMEM((2, most // 4, LANES), BF16),
        pltpu.VMEM((2, 16, most // 64, LANES), BF16),
        pltpu.VMEM((2, most // 64, LANES), BF16),
        pltpu.VMEM((groups, tiles * 2 * TILE, LANES), BF16),
        pltpu.VMEM((genes // TILE, TILE, 3 * TILE), BF16),
        *[pltpu.VMEM((genes, LANES), BF16)] * 3,
        pltpu.VMEM((genes, LANES), F32),
        pltpu.VMEM((3, share, cols), BF16),
        pltpu.VMEM(dosage.shape, jnp.int32),
        pltpu.VMEM(perm.shape, jnp.int32),
    ]
    each = len(CUTS)
    counts = [3, 5, 3, 3, 3, *[n * each for n in (6, 15, 15, 4, 8, 8)], 3]
    pairs = [dma((n,)) for n in counts for _ in range(2)]
    sizes = (len(plain), len(pairs), 1)
    white = pl.pallas_call(
        functools.partial(kernel, sizes, nulls * snps * lax.axis_size(SNP)),
        out_shape=jax.ShapeDtypeStruct((share * groups, cols), BF16),
        in_specs=[hbm, hbm, hbm, vmem],
        out_specs=vmem,
        scratch_shapes=[*plain, *pairs, dma((7,))],
        compiler_params=pltpu.CompilerParams(
            collective_id=0, has_side_effects=True, vmem_limit_bytes=60 << 20
        ),
        name="whitened_scores",
    )(dosage, pheno, perm, snp_weight[None, :])
    return white[:rows].reshape(copies, snps, cols)


def solution(mesh):
    finer = Mesh(mesh.devices.reshape(2, 2, 4, 8, 2), (*SAMP, *SNP))
    in_specs = (P(SNP, SAMP), P(SAMP, None), P(None, SAMP), P(SNP))
    return jax.shard_map(
        shards, mesh=finer, in_specs=in_specs, out_specs=P(None, SNP, SAMP), check_vma=False
    )
```

time: 116 us -> 104 us (0.90)
  Pallas kernels: 111 us -> 102 us
  local copies, waits for them, and re-layouts: 4.76 us -> 1.8 us
    pallas_call x1, Pallas kernels: 111 us -> 102 us  [shards(): pl.pallas_call(functools.partial(kernel, sizes, nulls * snps * lax.axis_s...]
    unnamed x6 -> x0, local copies, waits for them, and re-layouts: 3.2 us -> none
where the time goes in v5:
time: 104 us; the launch traced here: 103 us
  Pallas kernels  102 us (98%)
  local copies, waits for them, and re-layouts  1.8 us (2%)
    pallas_call x1, Pallas kernels, shards(): pl.pallas_call(functools.partial(kernel, sizes, nulls * snps * lax.axis_s...  102 us

profile of v5, /device:TPU:1, one launch (start us, length us, event | category | flops | bytes accessed | tf_op | source)
XLA Modules:
  0.0 103.4 jit_solution(9153184633426086781)
XLA Ops:
  0.0 101.6 %whitened_scores.1 = bf16[448,512]{1,0:T(8,128)(2,1)} custom-call(s32[48,512]{1,0:T(8,128)} %dosage.1, bf16[512,2048]{1,0:T(8,128)(2,1)} %pheno.1, s32[8,512]{1,0:T(8,128)} %perm.1, f32[1,48]{1,0:T(1,128)} %bitcast.2), custom_call_target="tpu_custom_call" | custom-call | tf_op jit(solution)/shard_map/whitened_scores/pallas_call | solution.py:562
  101.6 1.8 %slice.3 = bf16[432,512]{1,0:T(8,128)(2,1)} slice(bf16[448,512]{1,0:T(8,128)(2,1)} %whitened_scores.1), slice={[0:432], [0:512]} | slice | bytes 884736 | tf_op jit(solution)/shard_map/slice | solution.py:573

commit v6 on v5

--- a/solution.py
+++ b/solution.py
@@ -28,7 +28,7 @@
 
 class Sender:
     def __init__(self):
-        self.started = []
+        self.started, self.older = [], []
 
     def __call__(self, src, dst, sems, i, there):
         copy = pltpu.make_async_remote_copy(
@@ -39,8 +39,13 @@
         self.started.append(copy)
         return copy
 
+    def settle(self):
+        for copy in self.older:
+            copy.wait_send()
+        self.started, self.older = [], self.started
+
     def finish(self):
-        for copy in self.started:
+        for copy in self.older + self.started:
             copy.wait_send()
 
 
@@ -205,25 +210,22 @@
 
 
 def spread_chunk(at, send, total, part, gram, scratch, k):
-    x_slots, pair, acc, slots, chunk, xr, rr, gr, xg, ys, cs, own_in, own_out = scratch
+    x_slots, acc, slots, chunk, xr, rr, gr, xg, ys, cs, own_in, own_out = scratch
     base, rows = (n * 2 * TILE for n in CUTS[k])
     block, half, bit = rows // 4, rows // 8, rows // 64
     x, z, y_hi = at.x, at.z, at.y_hi
     right, left, across = at.right, at.left, at.across
-    x_slots, pair, acc = x_slots.at[k], pair.at[k], acc.at[k]
+    x_slots, acc = x_slots.at[k], acc.at[k]
     slots, chunk = slots.at[k], chunk.at[k, pl.ds(0, bit)]
 
-    def half_of(owner, h):
-        return part.at[pl.ds(pl.multiple_of(base + owner * block + h * half, 64), half)]
-
     def slot(i):
-        return x_slots.at[i, pl.ds(0, half)]
+        return x_slots.at[i, pl.ds(0, block)]
 
     def x_sent(i, src, there):
-        return send(src, slot(i), xr, 6 * k + i, there)
+        return send(src, slot(i), xr, 3 * k + i, there)
 
     def added(dst, sources):
-        @pl.loop(0, half, step=64)
+        @pl.loop(0, block, step=64)
         def _(r):
             rows_at = pl.ds(pl.multiple_of(r, 64), 64)
             value = sources[0][rows_at, :].astype(F32)
@@ -231,27 +233,20 @@
                 value += source[rows_at, :].astype(F32)
             dst[rows_at, :] = value.astype(BF16)
 
-    def summed(h):
-        return pair.at[h, pl.ds(0, half)]
-
-    hop_r = x_sent(0, half_of(across, 0), at.to_right)
-    hop_l = x_sent(1, half_of(across, 1), at.to_left)
-    own_r = x_sent(2, half_of(right, 1), at.to_right)
-    own_l = x_sent(3, half_of(left, 0), at.to_left)
-    yield
-    hop_r.wait_recv()
-    added(summed(0), [half_of(right, 0), slot(0)])
-    sum_r = x_sent(4, summed(0), at.to_right)
-    hop_l.wait_recv()
-    added(summed(1), [half_of(left, 1), slot(1)])
-    sum_l = x_sent(5, summed(1), at.to_left)
-    yield
-    own_l.wait_recv()
-    sum_r.wait_recv()
-    added(acc.at[pl.ds(0, half)], [half_of(x, 0), slot(3), slot(4)])
-    own_r.wait_recv()
-    sum_l.wait_recv()
-    added(acc.at[pl.ds(half, half)], [half_of(x, 1), slot(2), slot(5)])
+    def block_of(owner):
+        return part.at[pl.ds(pl.multiple_of(base + owner * block, 128), block)]
+
+    across_way = {"x": across}
+    arrive = [
+        x_sent(i, block_of(owner), there)
+        for i, (owner, there) in enumerate(
+            ((across, across_way), (right, at.to_right), (left, at.to_left))
+        )
+    ]
+    yield
+    for copy in arrive:
+        copy.wait_recv()
+    added(acc.at[pl.ds(0, block)], [block_of(x), slot(0), slot(1), slot(2)])
 
     def bit_at(at_y, at_z):
         return acc.at[pl.ds(pl.multiple_of((at_y * 8 + at_z) * bit, 16), bit)]
@@ -292,7 +287,7 @@
         return gram.at[which, pl.ds(pl.multiple_of(base + owner * block, 128), block)]
 
     def to_x(i, src, there):
-        return send(src, src, xg, 4 * k + i, there)
+        return send(src, src, xg, 3 * k + i, there)
 
     c_all = []
 
@@ -303,38 +298,26 @@
     def to_y(i, owner, h):
         src = at_half(piece, owner, h)
         return send(src, src, ys, 8 * k + 2 * i + h, at.far if h else at.near)
-
-    go_r = to_x(0, at_block(piece, x), at.to_right)
-    go_l = to_x(1, at_block(piece, x), at.to_left)
-    y_own = [to_y(0, x, h) for h in range(2)]
-    to_sibling(piece, x)
-    yield
-    go_r.wait_recv()
-    hop_r = to_x(2, at_half(piece, left, 0), at.to_right)
-    y_left = [to_y(1, left, h) for h in range(2)]
-    go_l.wait_recv()
-    hop_l = to_x(3, at_half(piece, right, 1), at.to_left)
-    y_right = [to_y(2, right, h) for h in range(2)]
-    to_sibling(piece, left)
-    to_sibling(piece, right)
 
     def from_y(copies, owner):
         for copy in copies:
             copy.wait_recv()
         to_sibling(at.near_id, owner)
 
-    yield
-    hop_r.wait_recv()
-    y_far = [to_y(3, across, 0)]
-    hop_l.wait_recv()
-    y_far.append(to_y(3, across, 1))
-    to_sibling(piece, across)
+    ways = ((at.to_right, left), (at.to_left, right), (across_way, across))
+    x_coming = [to_x(i, at_block(piece, x), there) for i, (there, _) in enumerate(ways)]
+    y_own = [to_y(0, x, h) for h in range(2)]
+    to_sibling(piece, x)
+    yield
+    y_coming = []
+    for i, (copy, (_, owner)) in enumerate(zip(x_coming, ways)):
+        copy.wait_recv()
+        y_coming.append([to_y(i + 1, owner, h) for h in range(2)])
+        to_sibling(piece, owner)
     from_y(y_own, x)
     yield
-    from_y(y_left, left)
-    from_y(y_right, right)
-    yield
-    from_y(y_far, across)
+    for copies, (_, owner) in zip(y_coming, ways):
+        from_y(copies, owner)
     yield
     for copy in c_all:
         copy.wait_recv()
@@ -453,6 +436,7 @@
                 leaving[t, :, cols_at] = value
         if there is not None:
             coming.append(send(leaving.at[t], out.at[mine], os, t, there))
+    send.settle()
     for copy in coming:
         copy.wait_recv()
     yield
@@ -467,12 +451,13 @@
     pairs = [(pairs[i], pairs[i + 1]) for i in range(0, len(pairs), 2)]
     (
         coded, codes, placed, cols_in, turned, near_w, part, every,
-        x_slots, pair, acc, slots, chunk, gram, lower, start, first, second, partial, leaving,
+        x_slots, acc, slots, chunk, gram, lower, start, first, second, partial, leaving,
         dose_here, perm_here,
     ) = plain
     at, send = Place(), Sender()
     barrier = pltpu.get_barrier_semaphore()
-    greeted = [at.sibling, at.near, at.cross, at.far, at.far_cross, at.to_right, at.to_left]
+    greeted = [at.sibling, at.near, at.cross, at.far, at.far_cross]
+    greeted += [at.to_right, at.to_left, {"x": at.across}]
     greeted += [at.peer(*p) for p in at.peers]
     for there in greeted:
         pl.semaphore_signal(barrier, inc=1, device_id=there, device_id_type=MESH)
@@ -496,24 +481,28 @@
         (coded, codes, placed, cols_in, turned, near_w, *pairs[:5], singles.at[0]),
     )
     moved = (
-        x_slots, pair, acc, slots, chunk, *pairs[5:11], singles.at[pl.ds(3, 2)], singles.at[pl.ds(5, 2)],
+        x_slots, acc, slots, chunk, *pairs[5:11], singles.at[pl.ds(3, 2)], singles.at[pl.ds(5, 2)],
     )
     here, cross = (spread_chunk(at, send, total, part, gram, moved, k) for k in range(2))
     white = white_steps(
         at, send, pheno.shape[1], gram, every, out,
         (lower, start, first, second, partial, leaving, pairs[11]),
     )
-    for _ in range(3):
-        next(scores)
-        next(here)
+    next(scores)
+    next(here)
+    next(scores)
+    send.settle()
+    next(here)
+    next(scores)
     next(scores)
     next(cross)
     next(white)
     for _ in here:
+        send.settle()
         next(cross)
     next(white)
     for _ in cross:
-        pass
+        send.settle()
     next(white)
     send.finish()
 
@@ -542,8 +531,7 @@
         pltpu.VMEM((rows - snps, 3 * cols), BF16),
         pltpu.VMEM((tiles * 2 * TILE, LANES), BF16),
         pltpu.VMEM((groups, share * groups, cols), BF16),
-        pltpu.VMEM((2, 6, most // 8, LANES), BF16),
-        pltpu.VMEM((2, 2, most // 8, LANES), BF16),
+        pltpu.VMEM((2, 3, most // 4, LANES), BF16),
         pltpu.VMEM((2, most // 4, LANES), BF16),
         pltpu.VMEM((2, 16, most // 64, LANES), BF16),
         pltpu.VMEM((2, most // 64, LANES), BF16),
@@ -556,7 +544,7 @@
         pltpu.VMEM(perm.shape, jnp.int32),
     ]
     each = len(CUTS)
-    counts = [3, 5, 3, 3, 3, *[n * each for n in (6, 15, 15, 4, 8, 8)], 3]
+    counts = [3, 5, 3, 3, 3, *[n * each for n in (3, 15, 15, 3, 8, 8)], 3]
     pairs = [dma((n,)) for n in counts for _ in range(2)]
     sizes = (len(plain), len(pairs), 1)
     white = pl.pallas_call(

time: 104 us -> 96.6 us (0.929)
  Pallas kernels: 102 us -> 94.7 us
    pallas_call x1, Pallas kernels: 102 us -> 94.7 us  [shards(): pl.pallas_call(functools.partial(kernel, sizes, nulls * snps * lax.axis_s...]
where the time goes in v6:
time: 96.6 us; the launch traced here: 96.5 us
  Pallas kernels  94.7 us (98%)
  local copies, waits for them, and re-layouts  1.8 us (2%)
    pallas_call x1, Pallas kernels, shards(): pl.pallas_call(functools.partial(kernel, sizes, nulls * snps * lax.axis_s...  94.7 us

profile of v6, /device:TPU:1, one launch (start us, length us, event | category | flops | bytes accessed | tf_op | source)
XLA Modules:
  0.0 96.5 jit_solution(8682157975968241425)
XLA Ops:
  0.0 94.7 %whitened_scores.1 = bf16[448,512]{1,0:T(8,128)(2,1)} custom-call(s32[48,512]{1,0:T(8,128)} %dosage.1, bf16[512,2048]{1,0:T(8,128)(2,1)} %pheno.1, s32[8,512]{1,0:T(8,128)} %perm.1, f32[1,48]{1,0:T(1,128)} %bitcast.2), custom_call_target="tpu_custom_call" | custom-call | tf_op jit(solution)/shard_map/whitened_scores/pallas_call | solution.py:550
  94.7 1.8 %slice.3 = bf16[432,512]{1,0:T(8,128)(2,1)} slice(bf16[448,512]{1,0:T(8,128)(2,1)} %whitened_scores.1), slice={[0:432], [0:512]} | slice | bytes 884736 | tf_op jit(solution)/shard_map/slice | solution.py:561

commit v7 on v6

--- a/solution.py
+++ b/solution.py
@@ -66,7 +66,8 @@
         self.right, self.left = lax.rem(x + 1, 4), lax.rem(x + 3, 4)
         self.across = lax.rem(x + 2, 4)
         self.to_right, self.to_left = {"x": self.right}, {"x": self.left}
-        self.peers = [(dz, dy) for dz in range(8) for dy in range(2) if dz or dy]
+        peers = [(dz, dy) for dz in range(8) for dy in range(2) if dz or dy]
+        self.peers = sorted(peers, key=lambda p: -min(p[0], 8 - p[0]) - 2 * p[1])
 
     def peer(self, dz, dy):
         there = {"z": lax.rem(self.z + dz, 8)}
@@ -397,19 +398,28 @@
         for i in range(2):
             partial[span(2 * a + i, TILE), :] = on_chip(start, a, i)
 
-    yield
+    def absorb(a):
+        for i in range(2):
+            direct = places(a, i)[2]
+            for t in range(2):
+                row = 6 + i * 2 + t
+                turned = flipped(a, row)
+                lower[2 * direct + t, :, (i + 1) * TILE : (i + 2) * TILE] = turned
+                partial[span(2 * a + i, TILE), :] += product(strip(a, row), start, 2 * direct + t)
+                partial[span(2 * direct + t, TILE), :] += product(turned, start, 2 * a + i)
+
+    yield
+    absorb(at.me)
+    yield
+    absorb(at.near_id)
+    yield
+    absorb(at.sib_id)
+    absorb(at.cross_id)
 
     @pl.loop(0, pieces)
     def _(a):
         for i in range(2):
-            direct = places(a, i)[2]
-            for t in range(2):
-                lower[2 * direct + t, :, (i + 1) * TILE : (i + 2) * TILE] = flipped(a, 6 + i * 2 + t)
-
-    @pl.loop(0, pieces)
-    def _(a):
-        for i in range(2):
-            value = (partial[span(2 * a + i, TILE), :] + off_chip(start, a, i)) * inverse
+            value = partial[span(2 * a + i, TILE), :] * inverse
             first[span(2 * a + i, TILE), :] = (1.5 * own(start, a, i) - 0.5 * value).astype(BF16)
 
     @pl.loop(0, pieces)
@@ -501,8 +511,10 @@
         send.settle()
         next(cross)
     next(white)
+    next(white)
     for _ in cross:
         send.settle()
+        next(white)
     next(white)
     send.finish()
 

time: 96.6 us -> 93.2 us (0.965)
  Pallas kernels: 94.7 us -> 91.2 us
    pallas_call x1, Pallas kernels: 94.7 us -> 91.2 us  [shards(): pl.pallas_call(functools.partial(kernel, sizes, nulls * snps * lax.axis_s...]
where the time goes in v7:
time: 93.2 us; the launch traced here: 93 us
  Pallas kernels  91.2 us (98%)
  local copies, waits for them, and re-layouts  1.8 us (2%)
    pallas_call x1, Pallas kernels, shards(): pl.pallas_call(functools.partial(kernel, sizes, nulls * snps * lax.axis_s...  91.2 us

profile of v7, /device:TPU:1, one launch (start us, length us, event | category | flops | bytes accessed | tf_op | source)
XLA Modules:
  0.0 93.0 jit_solution(17607028789955365166)
XLA Ops:
  0.0 91.2 %whitened_scores.1 = bf16[448,512]{1,0:T(8,128)(2,1)} custom-call(s32[48,512]{1,0:T(8,128)} %dosage.1, bf16[512,2048]{1,0:T(8,128)(2,1)} %pheno.1, s32[8,512]{1,0:T(8,128)} %perm.1, f32[1,48]{1,0:T(1,128)} %bitcast.2), custom_call_target="tpu_custom_call" | custom-call | tf_op jit(solution)/shard_map/whitened_scores/pallas_call | solution.py:562
  91.2 1.8 %slice.3 = bf16[432,512]{1,0:T(8,128)(2,1)} slice(bf16[448,512]{1,0:T(8,128)(2,1)} %whitened_scores.1), slice={[0:432], [0:512]} | slice | bytes 884736 | tf_op jit(solution)/shard_map/slice | solution.py:573

commit v8 on v7

--- a/solution.py
+++ b/solution.py
@@ -314,6 +314,7 @@
     for i, (copy, (_, owner)) in enumerate(zip(x_coming, ways)):
         copy.wait_recv()
         y_coming.append([to_y(i + 1, owner, h) for h in range(2)])
+    for _, owner in ways:
         to_sibling(piece, owner)
     from_y(y_own, x)
     yield
@@ -442,10 +443,10 @@
             cols_at = slice(i * TILE, (i + 1) * TILE)
             if there is None:
                 out[mine, cols_at] = value
-            else:
-                leaving[t, :, cols_at] = value
-        if there is not None:
-            coming.append(send(leaving.at[t], out.at[mine], os, t, there))
+                continue
+            leaving[t, :, cols_at] = value
+            dst = out.at[mine, cols_at]
+            coming.append(send(leaving.at[t, :, cols_at], dst, os, 2 * t + i, there))
     send.settle()
     for copy in coming:
         copy.wait_recv()
@@ -466,9 +467,9 @@
     ) = plain
     at, send = Place(), Sender()
     barrier = pltpu.get_barrier_semaphore()
-    greeted = [at.sibling, at.near, at.cross, at.far, at.far_cross]
-    greeted += [at.to_right, at.to_left, {"x": at.across}]
-    greeted += [at.peer(*p) for p in at.peers]
+    greeted = [at.peer(*p) for p in at.peers]
+    greeted += [{"x": at.across}, at.to_right, at.to_left]
+    greeted += [at.far_cross, at.far, at.cross, at.near, at.sibling]
     for there in greeted:
         pl.semaphore_signal(barrier, inc=1, device_id=there, device_id_type=MESH)
     snps, own = dosage.shape
@@ -556,7 +557,7 @@
         pltpu.VMEM(perm.shape, jnp.int32),
     ]
     each = len(CUTS)
-    counts = [3, 5, 3, 3, 3, *[n * each for n in (3, 15, 15, 3, 8, 8)], 3]
+    counts = [3, 5, 3, 3, 3, *[n * each for n in (3, 15, 15, 3, 8, 8)], 6]
     pairs = [dma((n,)) for n in counts for _ in range(2)]
     sizes = (len(plain), len(pairs), 1)
     white = pl.pallas_call(

time: 93.2 us -> 93 us (level)
  no operation moved by 1% of the time
where the time goes in v8:
time: 93 us; the launch traced here: 92.8 us
  Pallas kernels  91 us (98%)
  local copies, waits for them, and re-layouts  1.8 us (2%)
    pallas_call x1, Pallas kernels, shards(): pl.pallas_call(functools.partial(kernel, sizes, nulls * snps * lax.axis_s...  91 us

profile of v8, /device:TPU:1, one launch (start us, length us, event | category | flops | bytes accessed | tf_op | source)
XLA Modules:
  0.0 92.8 jit_solution(4426016948429070593)
XLA Ops:
  0.0 91.0 %whitened_scores.1 = bf16[448,512]{1,0:T(8,128)(2,1)} custom-call(s32[48,512]{1,0:T(8,128)} %dosage.1, bf16[512,2048]{1,0:T(8,128)(2,1)} %pheno.1, s32[8,512]{1,0:T(8,128)} %perm.1, f32[1,48]{1,0:T(1,128)} %bitcast.2), custom_call_target="tpu_custom_call" | custom-call | tf_op jit(solution)/shard_map/whitened_scores/pallas_call | solution.py:563
  91.0 1.8 %slice.3 = bf16[432,512]{1,0:T(8,128)(2,1)} slice(bf16[448,512]{1,0:T(8,128)(2,1)} %whitened_scores.1), slice={[0:432], [0:512]} | slice | bytes 884736 | tf_op jit(solution)/shard_map/slice | solution.py:574

commit v9 on v8

--- a/solution.py
+++ b/solution.py
@@ -77,7 +77,7 @@
 
 
 def score_steps(at, send, dosage, pheno, snp_weight, part, every, scratch):
-    coded, codes, placed, cols_in, turned, near_w, a, p, s, n, f, own_sem = scratch
+    coded, codes, placed, cols_in, early, turned, near_w, a, p, s, n, f, own_sem = scratch
     snps, own = dosage.shape
     samples, cols = cols_in.shape
     nulls = codes.shape[0] // 2
@@ -137,7 +137,11 @@
         for h in range(steps):
             placed[rows, h * LOW : (h + 1) * LOW] = got[h * snps : (h + 1) * snps]
 
+    half = samples // 2
+    here, there = span(at.y_lo, half), span(1 - at.y_lo, half)
     stay.wait()
+    pheno_coming.pop().wait_recv()
+    early[...] = jnp.dot(placed[:, here], cols_in[here, :], preferred_element_type=F32)
     for copy in pheno_coming:
         copy.wait_recv()
 
@@ -147,7 +151,8 @@
     for c in range(CHUNKS):
         first = 0 if c == 0 else LEAD + c * per * snps
         last = LEAD + (c + 1) * per * snps
-        raw = jnp.dot(placed[first:last, :], cols_in[...], preferred_element_type=F32)
+        raw = early[first:last, :]
+        raw += jnp.dot(placed[first:last, there], cols_in[there, :], preferred_element_type=F32)
         if c == 0:
             total = raw[:1]
             raw = raw[LEAD:]
@@ -461,7 +466,7 @@
     plain, pairs, (singles,) = refs
     pairs = [(pairs[i], pairs[i + 1]) for i in range(0, len(pairs), 2)]
     (
-        coded, codes, placed, cols_in, turned, near_w, part, every,
+        coded, codes, placed, cols_in, early, turned, near_w, part, every,
         x_slots, acc, slots, chunk, gram, lower, start, first, second, partial, leaving,
         dose_here, perm_here,
     ) = plain
@@ -489,7 +494,7 @@
     pl.semaphore_wait(barrier, len(greeted))
     scores = score_steps(
         at, send, dosage, pheno, snp_weight, part, every,
-        (coded, codes, placed, cols_in, turned, near_w, *pairs[:5], singles.at[0]),
+        (coded, codes, placed, cols_in, early, turned, near_w, *pairs[:5], singles.at[0]),
     )
     moved = (
         x_slots, acc, slots, chunk, *pairs[5:11], singles.at[pl.ds(3, 2)], singles.at[pl.ds(5, 2)],
@@ -540,6 +545,7 @@
         pltpu.VMEM((2 * nulls, samples), F32),
         pltpu.VMEM((LEAD + rows, samples), BF16),
         pltpu.VMEM((samples, cols), BF16),
+        pltpu.VMEM((LEAD + rows, cols), F32),
         pltpu.VMEM((cols, rows - snps), BF16),
         pltpu.VMEM((rows - snps, 3 * cols), BF16),
         pltpu.VMEM((tiles * 2 * TILE, LANES), BF16),

time: 93 us -> 92.5 us (level)
  no operation moved by 1% of the time
where the time goes in v9:
time: 92.5 us; the launch traced here: 92.3 us
  Pallas kernels  90.5 us (98%)
  local copies, waits for them, and re-layouts  1.8 us (2%)
    pallas_call x1, Pallas kernels, shards(): pl.pallas_call(functools.partial(kernel, sizes, nulls * snps * lax.axis_s...  90.5 us

profile of v9, /device:TPU:1, one launch (start us, length us, event | category | flops | bytes accessed | tf_op | source)
XLA Modules:
  0.0 92.3 jit_solution(11059776563658560413)
XLA Ops:
  0.0 90.5 %whitened_scores.1 = bf16[448,512]{1,0:T(8,128)(2,1)} custom-call(s32[48,512]{1,0:T(8,128)} %dosage.1, bf16[512,2048]{1,0:T(8,128)(2,1)} %pheno.1, s32[8,512]{1,0:T(8,128)} %perm.1, f32[1,48]{1,0:T(1,128)} %bitcast.2), custom_call_target="tpu_custom_call" | custom-call | tf_op jit(solution)/shard_map/whitened_scores/pallas_call | solution.py:569
  90.5 1.8 %slice.3 = bf16[432,512]{1,0:T(8,128)(2,1)} slice(bf16[448,512]{1,0:T(8,128)(2,1)} %whitened_scores.1), slice={[0:432], [0:512]} | slice | bytes 884736 | tf_op jit(solution)/shard_map/slice | solution.py:580
